TPU v7x, 512 devices: a whole 4x8x8 slice. The times are simulated.
512 devices in a mesh: frame: 32 (over x, y), row: 16 (over z, core).
Axes of the slice: x: 4, y: 8, z: 8, core: 2. Of those that a mesh axis runs over, the one named last changes fastest.
Arguments:
- query_tok: bfloat16 [32, 128, 16, 2560], P('frame', 'row'), may hold values from -6 to 6
- key_tok: bfloat16 [32, 128, 16, 2560], P('frame', 'row'), may hold values from -6 to 6
- value_tok: bfloat16 [32, 128, 16, 2560], P('frame', 'row'), may hold values from -6 to 6
- grad_out: bfloat16 [32, 128, 16, 2560], P('frame', 'row'), may hold values from -6 to 6
- head_reach: int32 [20], replicated, may hold values from 0 to 1
- tile_offset: int32 [32, 32], P(None, 'row'), may hold values from -1 to 0
Outputs:
- grad_query: bfloat16 [32, 128, 16, 2560], P('frame', 'row')
- grad_key: bfloat16 [32, 128, 16, 2560], P('frame', 'row')
- grad_value: bfloat16 [32, 128, 16, 2560], P('frame', 'row')
All inputs are finite; a program needn't handle non-finite values.
Results may differ from a plain program's by a relative error of at most 0.011.
Values may be sent and summed in bfloat16 or wider, within the bound.
No kernel may reach another device: no remote copies, remote signals or barrier semaphores. Data moves between devices by JAX's collectives and lax.ppermute only.
A program may use at most 64 MiB of HBM per device.

v0:
```python
import math

import jax
import jax.numpy as jnp
from jax import lax
from jax.sharding import PartitionSpec as P


def from_behind(block, axis, distance):
    devices = range(lax.axis_size(axis))
    route = [(i - distance, i) for i in devices if i - distance in devices]
    return lax.ppermute(block, axis, route)


def extended_2(block, sides, width):
    for axis, dim in sides:
        count = lax.axis_size(axis)
        forward = [(i, i + 1) for i in range(count - 1)]
        backward = [(target, source) for source, target in forward]
        low = lax.ppermute(
            lax.slice_in_dim(block, block.shape[dim] - width, None, axis=dim), axis, forward
        )
        high = lax.ppermute(lax.slice_in_dim(block, 0, width, axis=dim), axis, backward)
        block = jnp.concatenate([low, block, high], axis=dim)
    return block


def make_windows(extended, frames):
    rows_dev = extended.shape[1] - 2
    tiles = rows_dev // 4
    width = extended.shape[2]
    trailing = extended.shape[3:]
    tail = [(0, 0)] * len(trailing)
    padded = jnp.pad(extended, [(0, 0), (0, 2), (0, 0)] + tail)
    upper_part = padded[:, 0:rows_dev].reshape((frames + 2, tiles, 4, width) + trailing)
    lower_part = padded[:, 4 : rows_dev + 4].reshape((frames + 2, tiles, 4, width) + trailing)[
        :, :, 0:2
    ]
    six_rows = jnp.concatenate([upper_part, lower_part], axis=2)
    stacked = jnp.stack([six_rows[step : step + frames] for step in range(3)], axis=2)
    return stacked.reshape((frames * tiles, 18 * width) + trailing)


def fold_terms(term, frames, rows_dev, width):
    tiles = rows_dev // 4
    trailing = term.shape[2:]
    tail = [(0, 0)] * len(trailing)
    grid = term.reshape((frames, tiles, 3, 6, width) + trailing)
    total = None
    for step in range(3):
        part = grid[:, :, step]
        first = part[:, :, 0:4].reshape((frames, rows_dev, width) + trailing)
        second = jnp.pad(part[:, :, 4:6], [(0, 0), (0, 0), (0, 2), (0, 0)] + tail).reshape(
            (frames, rows_dev, width) + trailing
        )
        rows_sum = (
            jnp.pad(first, [(0, 0), (0, 2), (0, 0)] + tail)
            + jnp.pad(second, [(0, 0), (4, 0), (0, 0)] + tail)[:, 0 : rows_dev + 2]
        )
        placed = jnp.pad(rows_sum, [(step, 2 - step)] + [(0, 0)] * (rows_sum.ndim - 1))
        total = placed if total is None else total + placed
    return total


def window_allowed(
    first_frame, frames, offsets, reach_on, row_dev, rows_dev, row_count, frame_count, width
):
    tiles = rows_dev // 4
    slots = reach_on.shape[0]
    tile_ids = jnp.arange(tiles)[:, None]
    win_rows = jnp.arange(6)[None, :]
    global_row = row_dev * rows_dev + 4 * tile_ids + win_rows - 1
    offset3 = offsets[:, :, None]
    rows_ok = (global_row >= 0) & (global_row < row_count)
    rows_ok = (
        rows_ok[None] & ((win_rows != 0) | (offset3 == -1)) & ((win_rows != 5) | (offset3 == 0))
    )
    frame_ids = first_frame + jnp.arange(frames)[:, None] + jnp.arange(3)[None, :] - 1
    frames_ok = (frame_ids >= 0) & (frame_ids < frame_count)
    heads_ok = reach_on[:, None] | (jnp.arange(3)[None, :] == 1)
    allow = (
        frames_ok[:, None, None, :, None]
        & heads_ok[None, None, :, :, None]
        & rows_ok[:, :, None, None, :]
    )
    allow = jnp.broadcast_to(allow[..., None], (frames, tiles, slots, 3, 6, width))
    return allow.reshape(frames * tiles, slots, 1, 18 * width)


def tile_attend(query_t, grad_t, key_w, value_w, allowed):
    head_dim = query_t.shape[3]
    inv_root = 1.0 / math.sqrt(head_dim)
    scores = (
        jnp.einsum("bqmd,bkmd->bmqk", query_t, key_w, preferred_element_type=jnp.float32) * inv_root
    )
    scores = jnp.where(allowed, scores, -1e30)
    top = jnp.max(scores, axis=-1, keepdims=True)
    expo = jnp.exp(scores - top)
    probs = expo / jnp.sum(expo, axis=-1, keepdims=True)
    weights = probs.astype(jnp.bfloat16)
    attended = jnp.einsum("bmqk,bkmd->bqmd", weights, value_w, preferred_element_type=jnp.float32)
    delta = jnp.transpose(jnp.sum(grad_t.astype(jnp.float32) * attended, axis=-1), (0, 2, 1))
    dprobs = jnp.einsum("bqmd,bkmd->bmqk", grad_t, value_w, preferred_element_type=jnp.float32)
    dscores = (probs * (dprobs - delta[..., None]) * inv_root).astype(jnp.bfloat16)
    grad_query = jnp.einsum(
        "bmqk,bkmd->bqmd", dscores, key_w, preferred_element_type=jnp.float32
    ).astype(jnp.bfloat16)
    key_term = jnp.einsum("bmqk,bqmd->bkmd", dscores, query_t, preferred_element_type=jnp.float32)
    value_term = jnp.einsum("bmqk,bqmd->bkmd", weights, grad_t, preferred_element_type=jnp.float32)
    return (grad_query, key_term, value_term)


def return_rims(whole):
    rows_dev = whole.shape[1] - 2
    rim_low = whole[:, 0].astype(jnp.bfloat16)
    rim_high = whole[:, rows_dev + 1].astype(jnp.bfloat16)
    from_above = from_behind(rim_low, "row", -1)
    from_below = from_behind(rim_high, "row", 1)
    own_rows = whole[:, 1 : rows_dev + 1]
    first_row = own_rows[:, 0] + from_below.astype(jnp.float32)
    last_row = own_rows[:, rows_dev - 1] + from_above.astype(jnp.float32)
    joined = jnp.concatenate(
        [first_row[:, None], own_rows[:, 1 : rows_dev - 1], last_row[:, None]], axis=1
    )
    return joined.astype(jnp.bfloat16)


def on_device(query_tok, key_tok, value_tok, grad_out, head_reach, tile_offset):
    rows_dev, width, packed = (query_tok.shape[1], query_tok.shape[2], query_tok.shape[3])
    heads = head_reach.shape[0]
    head_dim = packed // heads
    tiles = rows_dev // 4
    frame_count = lax.axis_size("frame")
    row_count = lax.axis_size("row") * rows_dev
    row_dev = lax.axis_index("row")
    frame_dev = lax.axis_index("frame")
    reach_on = head_reach == 1
    query_grid = query_tok.reshape(tiles, 4 * width, heads, head_dim)
    grad_grid = grad_out.reshape(tiles, 4 * width, heads, head_dim)
    pair_grid = jnp.stack(
        [
            key_tok.reshape(1, rows_dev, width, heads, head_dim),
            value_tok.reshape(1, rows_dev, width, heads, head_dim),
        ],
        axis=3,
    )
    extended = extended_2(pair_grid, (("frame", 0), ("row", 1)), 1)
    windows = make_windows(extended, 1)
    offsets = lax.dynamic_slice_in_dim(tile_offset, frame_dev, 1, 0)
    allowed = window_allowed(
        frame_dev, 1, offsets, reach_on, row_dev, rows_dev, row_count, frame_count, width
    )
    grad_query, key_term, value_term = tile_attend(
        query_grid, grad_grid, windows[:, :, 0], windows[:, :, 1], allowed
    )
    folded = jnp.stack(
        [fold_terms(key_term, 1, rows_dev, width), fold_terms(value_term, 1, rows_dev, width)],
        axis=3,
    )
    from_next = from_behind(folded[0], "frame", -1)
    from_prev = from_behind(folded[2], "frame", 1)
    middle = folded[1] + from_next + from_prev
    pair_grad = return_rims(middle[None])
    grad_key = pair_grad[:, :, :, 0]
    grad_value = pair_grad[:, :, :, 1]
    return (
        grad_query.reshape(1, rows_dev, width, packed),
        grad_key.reshape(1, rows_dev, width, packed),
        grad_value.reshape(1, rows_dev, width, packed),
    )


def solution(mesh):
    return jax.shard_map(
        on_device,
        mesh=mesh,
        in_specs=(
            P("frame", "row", None, None),
            P("frame", "row", None, None),
            P("frame", "row", None, None),
            P("frame", "row", None, None),
            P(),
            P(None, "row"),
        ),
        out_specs=(
            P("frame", "row", None, None),
            P("frame", "row", None, None),
            P("frame", "row", None, None),
        ),
        check_vma=False,
    )
```

profile of v0, /device:TPU:199, one launch (start us, length us, event | category | flops | bytes accessed | tf_op | source)
XLA Modules:
  0.0 197.2 jit_solution(11396201429577753271)
XLA Ops:
  0.6 1.6 stack_reshape.6
  2.9 1.4 copy.66
  4.2 5.4 %collective-permute-start.1 = (bf16[1,8,16,2,20,128]{5,2,4,3,1,0:T(8,128)(2,1)}, bf16[1,8,16,2,20,128]{5,2,4,3,1,0:T(8,128)(2,1)}, u32[]{:S(2)}, u32[]{:S(2)}) collective-permute-start(bf16[1,8,16,2,20,128]{5,2,4,3,1,0:T(8,128)(2,1)} %copy.66), channel_id=1, source_target_pairs={{16,0},{32,16},{48,32},{64,48},{80,64},{96,80},{112,96},{128,112},... | collective-permute-start | bytes 3932168 | tf_op jit(solution)/shard_map/ppermute | solution.py:23
  9.6 1.9 collective-permute-start
  11.7 25.7 %collective-permute-done.1 = bf16[1,8,16,2,20,128]{5,2,4,3,1,0:T(8,128)(2,1)} collective-permute-done((bf16[1,8,16,2,20,128]{5,2,4,3,1,0:T(8,128)(2,1)}, bf16[1,8,16,2,20,128]{5,2,4,3,1,0:T(8,128)(2,1)}, u32[]{:S(2)}, u32[]{:S(2)}) %collective-permute-start.1) | collective-permute-done | bytes 1310752 | tf_op jit(solution)/shard_map/ppermute | solution.py:23
  37.4 1.7 copy.69
  39.1 4.2 %collective-permute-done = bf16[1,8,16,2,20,128]{5,2,4,3,1,0:T(8,128)(2,1)} collective-permute-done((bf16[1,8,16,2,20,128]{5,2,4,3,1,0:T(8,128)(2,1)}, bf16[1,8,16,2,20,128]{5,2,4,3,1,0:T(8,128)(2,1)}, u32[]{:S(2)}, u32[]{:S(2)}) %collective-permute-start) | collective-permute-done | bytes 1310752 | tf_op jit(solution)/shard_map/ppermute | solution.py:20
  43.3 1.7 copy.68
  45.2 1.1 copy.70
  46.3 0.8 copy.73
  47.2 3.7 %collective-permute-start.3 = (bf16[3,1,16,2,20,128]{5,2,4,3,1,0:T(8,128)(2,1)}, bf16[3,1,16,2,20,128]{5,2,4,3,1,0:T(8,128)(2,1)}, u32[]{:S(2)}, u32[]{:S(2)}) collective-permute-start(bf16[3,1,16,2,20,128]{5,2,4,3,1,0:T(8,128)(2,1)} %copy.73), channel_id=1, source_target_pairs={{1,0},{2,1},{3,2},{4,3},{5,4},{6,5},{7,6},{8,7},{9,8},{10,9},{11,1... | collective-permute-start | bytes 1474568 | tf_op jit(solution)/shard_map/ppermute | solution.py:23
  50.9 5.3 %collective-permute-start.2 = (bf16[3,1,16,2,20,128]{5,2,4,3,1,0:T(8,128)(2,1)}, bf16[3,1,16,2,20,128]{5,2,4,3,1,0:T(8,128)(2,1)}, u32[]{:S(2)}, u32[]{:S(2)}) collective-permute-start(bf16[3,1,16,2,20,128]{5,2,4,3,1,0:T(8,128)(2,1)} %copy.70), channel_id=1, source_target_pairs={{0,1},{1,2},{2,3},{3,4},{4,5},{5,6},{6,7},{7,8},{8,9},{9,10},{10,1... | collective-permute-start | bytes 1474568 | tf_op jit(solution)/shard_map/ppermute | solution.py:20
  57.1 2.2 %reshape.365 = bf16[2,64,20,128]{3,2,1,0:T(8,128)(2,1)} reshape(bf16[1,8,16,2560]{3,2,1,0:T(8,128)(2,1)} %param.9) | data formatting | bytes 1310720 | tf_op jit(solution)/shard_map/reshape | solution.py:139
  59.3 2.2 %reshape.364 = bf16[2,64,20,128]{3,2,1,0:T(8,128)(2,1)} reshape(bf16[1,8,16,2560]{3,2,1,0:T(8,128)(2,1)} %param.6) | data formatting | bytes 1310720 | tf_op jit(solution)/shard_map/reshape | solution.py:138
  61.5 1.2 copy.75
  62.7 1.2 copy.71
  63.9 4.9 %pad_maximum_fusion.1 = (bf16[3,8,16,2,20,128]{5,4,2,1,3,0:T(8,128)(2,1)S(1)}, bf16[3,8,16,2,20,128]{5,4,2,1,3,0:T(8,128)(2,1)S(1)}) fusion(bf16[3,1,16,2,20,128]{5,4,2,1,3,0:T(8,128)(2,1)S(1)} %copy.71, bf16[1,8,16,2,20,128]{5,4,2,1,3,0:T(8,128)(2,1)S(1)} %copy.69, bf16[1,8,16,2,20,128]{5,4,2,1,3,0:T(8,128)(2,1)S(1)} %constant_dynamic-update-slice_fusion, ...), kind=kLoop, calls=%fused_computation.22 | loop fusion | flops 49152000 | bytes 12779520 | tf_op jit(solution)/shard_map/concatenate | solution.py:24
  68.8 1.0 copy.72
  69.8 1.0 copy.76
  71.2 0.6 fusion.31
  71.8 0.7 pad_maximum_fusion
  72.5 1.1 copy.77
  73.6 1.2 fusion.25
  74.9 7.5 %fusion.67 = (f32[2,20,64]{2,1,0:T(8,128)S(1)}, f32[2,20,64,288]{3,2,1,0:T(8,128)S(1)}) fusion(f32[2,20,288,64]{2,3,1,0:T(8,128)S(1)} %fusion.25, pred[2,20,288]{2,1,0:T(8,128)(4,1)S(1)} %broadcast_in_dim.15), kind=kOutput, calls=%fused_computation.121 | output fusion | flops 4423967 | bytes 5920000 | tf_op jit(solution)/shard_map/sub | solution.py:98
  82.4 1.2 fusion.46
  83.7 1.6 fusion.51
  85.3 0.4 fusion.65
  86.9 1.7 fusion.11
  88.6 1.1 fusion.48
  89.9 0.4 fusion.64
  93.4 0.5 add_bitcast_fusion
  93.9 0.4 add_bitcast_fusion.1
  94.3 2.1 %fusion.15 = (f32[10,16,2,20,128]{4,1,3,0,2:T(8,128)}, f32[10,16,2,20,128]{4,1,3,0,2:T(8,128)S(1)}) fusion(f32[3,10,16,1,20,128]{5,2,4,1,0,3:T(8,128)S(1)} %add_bitcast_fusion.1, f32[3,10,16,1,20,128]{5,2,4,1,0,3:T(8,128)S(1)} %add_bitcast_fusion), kind=kLoop, calls=%fused_computation.34 | loop fusion | flops 1638400 | bytes 16384000 | tf_op jit(solution)/shard_map/squeeze | solution.py:160
  96.4 1.9 collective-permute-start.4
  98.3 3.4 %collective-permute-start.5 = (f32[10,16,2,20,128]{4,1,3,0,2:T(8,128)S(1)}, f32[10,16,2,20,128]{4,1,3,0,2:T(8,128)S(1)}, u32[]{:S(2)}, u32[]{:S(2)}) collective-permute-start(f32[10,16,2,20,128]{4,1,3,0,2:T(8,128)S(1)} %get-tuple-element.6), channel_id=1, source_target_pairs={{0,16},{16,32},{32,48},{48,64},{64,80},{80,96},{96,112},{112,128},... | collective-permute-start | bytes 9830408 | tf_op jit(solution)/shard_map/ppermute | solution.py:12
  101.7 68.8 %collective-permute-done.4 = f32[10,16,2,20,128]{4,1,3,0,2:T(8,128)S(1)} collective-permute-done((f32[10,16,2,20,128]{4,1,3,0,2:T(8,128)}, f32[10,16,2,20,128]{4,1,3,0,2:T(8,128)S(1)}, u32[]{:S(2)}, u32[]{:S(2)}) %collective-permute-start.4) | collective-permute-done | bytes 3276832 | tf_op jit(solution)/shard_map/ppermute | solution.py:12
  170.6 3.6 %collective-permute-done.5 = f32[10,16,2,20,128]{4,1,3,0,2:T(8,128)S(1)} collective-permute-done((f32[10,16,2,20,128]{4,1,3,0,2:T(8,128)S(1)}, f32[10,16,2,20,128]{4,1,3,0,2:T(8,128)S(1)}, u32[]{:S(2)}, u32[]{:S(2)}) %collective-permute-start.5) | collective-permute-done | bytes 3276832 | tf_op jit(solution)/shard_map/ppermute | solution.py:12
  174.2 0.6 fusion.20
  174.8 0.7 slice_bitcast_fusion.21
  175.5 4.5 %collective-permute-start.6 = (bf16[1,16,2,20,128]{4,1,3,2,0:T(8,128)(2,1)}, bf16[1,16,2,20,128]{4,1,3,2,0:T(8,128)(2,1)}, u32[]{:S(2)}, u32[]{:S(2)}) collective-permute-start(bf16[1,16,2,20,128]{4,1,3,2,0:T(8,128)(2,1)} %get-tuple-element.20), channel_id=1, source_target_pairs={{0,1},{1,2},{2,3},{3,4},{4,5},{5,6},{6,7},{7,8},{8,9},{9,10},{10,1... | collective-permute-start | bytes 491528 | tf_op jit(solution)/shard_map/ppermute | solution.py:12
  180.0 2.3 %fusion.47 = bf16[2,64,20,128]{3,1,2,0:T(8,128)(2,1)S(1)} fusion(bf16[2,20,64,288]{3,2,1,0:T(8,128)(2,1)} %copy-done.2, bf16[2,288,2,20,128]{4,1,3,0,2:T(8,128)(2,1)S(1)} %bitcast.156), kind=kOutput, calls=%fused_computation.82 | convolution fusion | flops 189071360 | bytes 5079040 | tf_op jit(solution)/shard_map/bmqk,bkmd->bqmd/dot_general | solution.py:105
  182.4 1.3 copy.82
  183.7 2.2 %reshape.366 = bf16[1,8,16,2560]{3,2,1,0:T(8,128)(2,1)} reshape(bf16[2,64,20,128]{3,2,1,0:T(8,128)(2,1)} %copy.82) | data formatting | bytes 1310720 | tf_op jit(solution)/shard_map/reshape | solution.py:167
  186.1 1.9 collective-permute-start.7
  188.2 1.0 fusion.58
  189.1 4.8 %collective-permute-done.7 = bf16[1,16,2,20,128]{4,1,3,2,0:T(8,128)(2,1)S(1)} collective-permute-done((bf16[1,16,2,20,128]{4,1,3,2,0:T(8,128)(2,1)S(1)}, bf16[1,16,2,20,128]{4,1,3,2,0:T(8,128)(2,1)S(1)}, u32[]{:S(2)}, u32[]{:S(2)}) %collective-permute-start.7) | collective-permute-done | bytes 163872 | tf_op jit(solution)/shard_map/ppermute | solution.py:12
  194.6 1.2 reshape_squeeze.7
  196.0 1.2 reshape_squeeze.6
  (70 shorter events, 7.6 us)
Async XLA Ops:
  0.6 1.7 copy-start.4
  2.3 9.3 %copy-start.6 = (s32[20]{0:T(128)S(1)}, s32[20]{0:T(128)}, u32[]{:S(2)}) copy-start(s32[20]{0:T(128)} %param.10) | copy-start | bytes 244
  4.2 33.1 %collective-permute-start.1 = (bf16[1,8,16,2,20,128]{5,2,4,3,1,0:T(8,128)(2,1)}, bf16[1,8,16,2,20,128]{5,2,4,3,1,0:T(8,128)(2,1)}, u32[]{:S(2)}, u32[]{:S(2)}) collective-permute-start(bf16[1,8,16,2,20,128]{5,2,4,3,1,0:T(8,128)(2,1)} %copy.66), channel_id=1, source_target_pairs={{16,0},{32,16},{48,32},{64,48},{80,64},{96,80},{112,96},{128,112},... | collective-permute-start | bytes 3932168 | tf_op jit(solution)/shard_map/ppermute | solution.py:23
  9.6 33.7 %collective-permute-start = (bf16[1,8,16,2,20,128]{5,2,4,3,1,0:T(8,128)(2,1)}, bf16[1,8,16,2,20,128]{5,2,4,3,1,0:T(8,128)(2,1)}, u32[]{:S(2)}, u32[]{:S(2)}) collective-permute-start(bf16[1,8,16,2,20,128]{5,2,4,3,1,0:T(8,128)(2,1)} %copy.66), channel_id=1, source_target_pairs={{0,16},{16,32},{32,48},{48,64},{64,80},{80,96},{96,112},{112,128},... | collective-permute-start | bytes 3932168 | tf_op jit(solution)/shard_map/ppermute | solution.py:20
  45.0 1.3 copy-start
  45.0 11.3 %copy-start.5 = (s32[32,2]{0,1:T(2,128)S(1)}, s32[32,2]{0,1:T(2,128)}, u32[]{:S(2)}) copy-start(s32[32,2]{0,1:T(2,128)} %param.11) | copy-start | bytes 772
  47.2 14.4 %collective-permute-start.3 = (bf16[3,1,16,2,20,128]{5,2,4,3,1,0:T(8,128)(2,1)}, bf16[3,1,16,2,20,128]{5,2,4,3,1,0:T(8,128)(2,1)}, u32[]{:S(2)}, u32[]{:S(2)}) collective-permute-start(bf16[3,1,16,2,20,128]{5,2,4,3,1,0:T(8,128)(2,1)} %copy.73), channel_id=1, source_target_pairs={{1,0},{2,1},{3,2},{4,3},{5,4},{6,5},{7,6},{8,7},{9,8},{10,9},{11,1... | collective-permute-start | bytes 1474568 | tf_op jit(solution)/shard_map/ppermute | solution.py:23
  50.9 11.8 %collective-permute-start.2 = (bf16[3,1,16,2,20,128]{5,2,4,3,1,0:T(8,128)(2,1)}, bf16[3,1,16,2,20,128]{5,2,4,3,1,0:T(8,128)(2,1)}, u32[]{:S(2)}, u32[]{:S(2)}) collective-permute-start(bf16[3,1,16,2,20,128]{5,2,4,3,1,0:T(8,128)(2,1)} %copy.70), channel_id=1, source_target_pairs={{0,1},{1,2},{2,3},{3,4},{4,5},{5,6},{6,7},{7,8},{8,9},{9,10},{10,1... | collective-permute-start | bytes 1474568 | tf_op jit(solution)/shard_map/ppermute | solution.py:20
  72.5 1.1 copy-start.1
  74.9 7.5 %copy-start.3 = (bf16[2,64,20,128]{3,2,1,0:T(8,128)(2,1)S(1)}, bf16[2,64,20,128]{3,2,1,0:T(8,128)(2,1)}, u32[]{:S(2)}) copy-start(bf16[2,64,20,128]{3,2,1,0:T(8,128)(2,1)} %reshape.365) | copy-start | bytes 1966084
  88.6 1.3 copy-start.2
  96.4 74.1 %collective-permute-start.4 = (f32[10,16,2,20,128]{4,1,3,0,2:T(8,128)}, f32[10,16,2,20,128]{4,1,3,0,2:T(8,128)S(1)}, u32[]{:S(2)}, u32[]{:S(2)}) collective-permute-start(f32[10,16,2,20,128]{4,1,3,0,2:T(8,128)} %get-tuple-element.5), channel_id=1, source_target_pairs={{16,0},{32,16},{48,32},{64,48},{80,64},{96,80},{112,96},{128,112},... | collective-permute-start | bytes 9830408 | tf_op jit(solution)/shard_map/ppermute | solution.py:12
  98.3 75.8 %collective-permute-start.5 = (f32[10,16,2,20,128]{4,1,3,0,2:T(8,128)S(1)}, f32[10,16,2,20,128]{4,1,3,0,2:T(8,128)S(1)}, u32[]{:S(2)}, u32[]{:S(2)}) collective-permute-start(f32[10,16,2,20,128]{4,1,3,0,2:T(8,128)S(1)} %get-tuple-element.6), channel_id=1, source_target_pairs={{0,16},{16,32},{32,48},{48,64},{64,80},{80,96},{96,112},{112,128},... | collective-permute-start | bytes 9830408 | tf_op jit(solution)/shard_map/ppermute | solution.py:12
  175.5 12.6 %collective-permute-start.6 = (bf16[1,16,2,20,128]{4,1,3,2,0:T(8,128)(2,1)}, bf16[1,16,2,20,128]{4,1,3,2,0:T(8,128)(2,1)}, u32[]{:S(2)}, u32[]{:S(2)}) collective-permute-start(bf16[1,16,2,20,128]{4,1,3,2,0:T(8,128)(2,1)} %get-tuple-element.20), channel_id=1, source_target_pairs={{0,1},{1,2},{2,3},{3,4},{4,5},{5,6},{6,7},{7,8},{8,9},{9,10},{10,1... | collective-permute-start | bytes 491528 | tf_op jit(solution)/shard_map/ppermute | solution.py:12
  186.1 7.8 %collective-permute-start.7 = (bf16[1,16,2,20,128]{4,1,3,2,0:T(8,128)(2,1)S(1)}, bf16[1,16,2,20,128]{4,1,3,2,0:T(8,128)(2,1)S(1)}, u32[]{:S(2)}, u32[]{:S(2)}) collective-permute-start(bf16[1,16,2,20,128]{4,1,3,2,0:T(8,128)(2,1)S(1)} %get-tuple-element.21), channel_id=1, source_target_pairs={{1,0},{2,1},{3,2},{4,3},{5,4},{6,5},{7,6},{8,7},{9,8},{10,9},{11,1... | collective-permute-start | bytes 491528 | tf_op jit(solution)/shard_map/ppermute | solution.py:12
where the time goes:
time: 198 us; the launch traced here: 197 us
  waiting for transfers between devices  107 us (54%)
  local copies, waits for them, and re-layouts  31.2 us (16%)
  starting transfers between devices  27.9 us (14%)
  other arithmetic  20.4 us (10%)
  matrix products  9.2 us (5%)
    ppermute x4, waiting for transfers between devices, from_behind(): return lax.ppermute(block, axis, route)  77.2 us
    ppermute x2, waiting for transfers between devices, extended_2(): lax.ppermute(lax.slice_in_dim(block, 0, width, axis=dim), axis, backward)  25.7 us
    ppermute x4, starting transfers between devices, from_behind(): return lax.ppermute(block, axis, route)  11.7 us
    ppermute x2, starting transfers between devices, extended_2(): lax.ppermute(lax.slice_in_dim(block, 0, width, axis=dim), axis, backward)  9.06 us
    sub x1, other arithmetic, tile_attend(): expo = jnp.exp(scores - top)  7.52 us
    ppermute x2, starting transfers between devices, extended_2(): lax.ppermute(lax.slice_in_dim(block, block.shape[dim] - width, None, axis...  7.21 us
    concatenate x1, other arithmetic, extended_2(): block = jnp.concatenate([low, block, high], axis=dim)  4.87 us
    ppermute x2, waiting for transfers between devices, extended_2(): lax.ppermute(lax.slice_in_dim(block, block.shape[dim] - width, None, axis...  4.23 us
  transfers between devices with their start and end apart: 8, of which 5 were waited for; matrix products, arithmetic and copies ran while one was open for 8% of the time, Pallas kernels for 0%

commit v1 on v0

v1 whole, which is shorter than its diff:
```python
import functools
import math

import jax
import jax.numpy as jnp
from jax import lax
from jax.experimental import pallas as pl
from jax.experimental.pallas import tpu as pltpu
from jax.sharding import PartitionSpec as P

STEP = 4
VMEM_LIMIT = 24 << 20
F32, BF16 = jnp.float32, jnp.bfloat16
SMEM = pl.BlockSpec(memory_space=pltpu.SMEM)
VMEM = pl.BlockSpec(memory_space=pltpu.VMEM)
ANY = pl.BlockSpec(memory_space=pl.ANY)


def shifted(block, axis, distance):
    devices = range(lax.axis_size(axis))
    route = [(i - distance, i) for i in devices if i - distance in devices]
    return lax.ppermute(block, axis, route)


def columns(head, dim):
    return pl.ds(pl.multiple_of(head * dim, dim), dim)


def dot_nt(a, b):
    return lax.dot_general(a, b, (((1,), (1,)), ((), ())), preferred_element_type=F32)


def dot_nn(a, b):
    return lax.dot_general(a, b, (((1,), (0,)), ((), ())), preferred_element_type=F32)


def dot_tn(a, b):
    return lax.dot_general(a, b, (((0,), (0,)), ((), ())), preferred_element_type=F32)


class Geometry:
    def __init__(self, tokens, width, dim):
        self.tokens, self.width, self.dim = tokens, width, dim
        self.half = tokens // 2
        self.frames = lax.axis_size("frame")
        self.frame = lax.axis_index("frame")
        self.row = lax.axis_index("row")
        self.rows = lax.axis_size("row")
        self.low_lanes = lax.broadcasted_iota(jnp.int32, (1, tokens), 1) < self.half

    def has(self, frame):
        return (frame >= 0) & (frame < self.frames)

    def offsets(self, offs_ref, frame):
        frame = jnp.clip(frame, 0, self.frames - 1)
        first, second = offs_ref[frame, 0], offs_ref[frame, 1]
        lost0 = (first == -1) & (self.row == 0)
        lost1 = (second == 0) & (self.row == self.rows - 1)
        fine, gone = jnp.float32(0.0), jnp.float32(-1e30)
        penalty = jnp.where(
            self.low_lanes, jnp.where(lost0, gone, fine), jnp.where(lost1, gone, fine)
        )
        return first == -1, second == -1, penalty

    def keys(self, main, low, high, offs):
        half, width = self.half, self.width
        edge0 = jnp.where(offs[0], low, main[half : half + width])
        edge1 = jnp.where(offs[1], main[half - width : half], high)
        return jnp.concatenate([main, edge0, edge1], axis=0)

    def by_tile(self, product):
        half, width, tokens = self.half, self.width, self.tokens
        own = jnp.where(self.low_lanes, product[:half], product[half:tokens])
        edge = jnp.where(
            self.low_lanes, product[tokens : tokens + width], product[tokens + width :]
        )
        return own, edge

    def scores(self, keys, values, query, grad, offs):
        own, edge = self.by_tile(dot_nt(keys, query))
        scale = 1.0 / math.sqrt(self.dim)
        s = jnp.concatenate([own * scale, edge * scale + offs[2]], axis=0)
        dp = jnp.concatenate(self.by_tile(dot_nt(values, grad)), axis=0)
        return s, dp

    def spread(self, terms):
        half = self.half
        own, edge = terms[:half], terms[half:]
        zero_own, zero_edge = jnp.zeros_like(own), jnp.zeros_like(edge)
        low = self.low_lanes
        return jnp.concatenate(
            [
                jnp.where(low, own, zero_own).astype(BF16),
                jnp.where(low, zero_own, own).astype(BF16),
                jnp.where(low, edge, zero_edge).astype(BF16),
                jnp.where(low, zero_edge, edge).astype(BF16),
            ],
            axis=0,
        )

    def grads(self, s, dp, keys, query, grad, top, inverse, delta):
        p = jnp.exp(s - top) * inverse
        ds = p * (dp - delta) * (1.0 / math.sqrt(self.dim))
        weights, dscores = self.spread(p), self.spread(ds)
        return dot_tn(dscores, keys), dot_nn(dscores, query), dot_nn(weights, grad)

    def fold(self, term, offs):
        half, width, tokens = self.half, self.width, self.tokens
        edge0, edge1 = term[tokens : tokens + width], term[tokens + width :]
        none = jnp.zeros_like(edge0)
        main = jnp.concatenate(
            [
                term[: half - width],
                term[half - width : half] + jnp.where(offs[1], edge1, none),
                term[half : half + width] + jnp.where(offs[0], none, edge0),
                term[half + width : tokens],
            ],
            axis=0,
        )
        return main, jnp.where(offs[0], edge0, none), jnp.where(offs[1], none, edge1)


def stats_of(s, dp):
    top = jnp.max(s, axis=0, keepdims=True)
    expo = jnp.exp(s - top)
    return top, jnp.sum(expo, axis=0, keepdims=True), jnp.sum(expo * dp, axis=0, keepdims=True)


def put_stats(ref, pair, side, stats):
    for j, row in enumerate(stats):
        ref[pair, pl.ds(4 * side + j, 1), :] = row


def get_stats(ref, pair, side):
    return [ref[pair, pl.ds(4 * side + j, 1), :] for j in range(3)]


def merge(first, others, valid):
    low = jnp.float32(-1e30)
    tops = [first[0]] + [jnp.where(ok, o[0], low) for o, ok in zip(others, valid)]
    top = functools.reduce(jnp.maximum, tops)
    factor = jnp.exp(first[0] - top)
    total, weighted = first[1] * factor, first[2] * factor
    for o, ok, t in zip(others, valid, tops[1:]):
        factor = jnp.where(ok, jnp.exp(t - top), jnp.float32(0.0))
        total, weighted = total + o[1] * factor, weighted + o[2] * factor
    inverse = 1.0 / total
    return top, inverse, weighted * inverse


def pack_kernel(n, heads, dim, width, reach, q, g, k, v, order, send, low, high, sems):
    tokens = q.shape[0]
    rim_copies = []
    for j, ref in enumerate((k, v)):
        rim_copies.append(pltpu.make_async_copy(ref.at[:width], low.at[j], sems.at[n, j]))
        rim_copies.append(
            pltpu.make_async_copy(ref.at[tokens - width :], high.at[j], sems.at[n + 1, j])
        )
    for copy in rim_copies:
        copy.start()
    count = lax.fori_loop(0, heads, lambda h, c: c + reach[h], 0)

    def place(h, carry):
        on, off = carry
        hit = reach[h] == 1
        order[jnp.where(hit, on, off)] = h
        return jnp.where(hit, on + 1, on), jnp.where(hit, off, off + 1)

    lax.fori_loop(0, heads, place, (0, count))

    def copies(slot):
        cols = columns(order[slot], dim)
        return [
            pltpu.make_async_copy(ref.at[:, cols], send.at[slot, j], sems.at[slot, j])
            for j, ref in enumerate((q, g))
        ]

    def start(slot, carry):
        for copy in copies(slot):
            copy.start()
        return carry

    def wait(slot, carry):
        for copy in copies(slot):
            copy.wait()
        return carry

    lax.fori_loop(0, n, start, 0)
    lax.fori_loop(0, n, wait, 0)
    for copy in rim_copies:
        copy.wait()


def own_kernel(
    n, heads, dim, width, order, offs, q, g, k, v, low, high,
    stats, dq, dk, dv, rim_low, rim_high, buf, rbuf, sems,
):
    geo = Geometry(q.shape[0], width, dim)
    where = geo.offsets(offs, geo.frame)

    def load(slot):
        cols = columns(order[slot], dim)
        keys = geo.keys(k[:, cols], low[0, :, cols], high[0, :, cols], where)
        values = geo.keys(v[:, cols], low[1, :, cols], high[1, :, cols], where)
        return keys, values, q[:, cols], g[:, cols]

    def partial(pair, carry):
        for side in range(2):
            keys, values, query, grad = load(2 * pair + side)
            put_stats(stats, pair, side, stats_of(*geo.scores(keys, values, query, grad, where)))
        return carry

    if n:
        lax.fori_loop(0, n // 2, partial, 0)

    def copies(slot):
        cols = columns(order[slot], dim)
        i = slot - n
        return [
            pltpu.make_async_copy(buf.at[i, j], ref.at[:, cols], sems.at[i, j])
            for j, ref in enumerate((dq, dk, dv))
        ] + [
            pltpu.make_async_copy(rbuf.at[i, j], ref.at[:, :, cols], sems.at[i, 3 + j])
            for j, ref in enumerate((rim_low, rim_high))
        ]

    def finish(pair, carry):
        for side in range(2):
            slot = n + 2 * pair + side
            keys, values, query, grad = load(slot)
            s, dp = geo.scores(keys, values, query, grad, where)
            top, total, weighted = stats_of(s, dp)
            inverse = 1.0 / total
            grad_q, grad_k, grad_v = geo.grads(
                s, dp, keys, query, grad, top, inverse, weighted * inverse
            )
            i = slot - n
            buf[i, 0] = grad_q.astype(BF16)
            for j, term in enumerate((grad_k, grad_v)):
                main, below, above = geo.fold(term, where)
                buf[i, 1 + j] = main.astype(BF16)
                rbuf[i, 0, j] = below.astype(BF16)
                rbuf[i, 1, j] = above.astype(BF16)
            for copy in copies(slot):
                copy.start()
        return carry

    def wait(slot, carry):
        for copy in copies(slot):
            copy.wait()
        return carry

    if n < heads:
        lax.fori_loop(0, (heads - n) // 2, finish, 0)
        lax.fori_loop(n, heads, wait, 0)


def near_kernel(n, dim, width, order, offs, k, v, low, high, prev, following, s_prev, s_next):
    geo = Geometry(k.shape[0], width, dim)

    def pair_step(pair, carry):
        for side in range(2):
            slot = 2 * pair + side
            cols = columns(order[slot], dim)
            for step, near, out in ((-1, prev, s_prev), (1, following, s_next)):
                where = geo.offsets(offs, geo.frame + step)
                keys = geo.keys(k[:, cols], low[0, :, cols], high[0, :, cols], where)
                values = geo.keys(v[:, cols], low[1, :, cols], high[1, :, cols], where)
                s, dp = geo.scores(keys, values, near[slot, 0], near[slot, 1], where)
                put_stats(out, pair, side, stats_of(s, dp))
        return carry

    lax.fori_loop(0, n // 2, pair_step, 0)


def main_kernel(
    n, dim, width, order, reach, offs, q, g, k, v, low, high, prev, following,
    own, own_prev, own_next, near_prev, near_next, at_prev, at_next, far_prev, far_next,
    dk_in, dv_in, rim_low_in, rim_high_in,
    dq_own, dq_prev, dq_next, dk, dv, rim_low, rim_high, buf, rbuf, sems,
):
    del dk_in, dv_in, rim_low_in, rim_high_in
    geo = Geometry(q.shape[0], width, dim)
    f = geo.frame

    def copies(slot):
        cols = columns(order[slot], dim)
        return [
            pltpu.make_async_copy(buf.at[slot, j], ref.at[:, cols], sems.at[slot, j])
            for j, ref in enumerate((dk, dv))
        ] + [
            pltpu.make_async_copy(rbuf.at[slot, j], ref.at[:, :, cols], sems.at[slot, 2 + j])
            for j, ref in enumerate((rim_low, rim_high))
        ]

    def pair_step(pair, carry):
        for side in range(2):
            slot = 2 * pair + side
            head = order[slot]
            on = reach[head] == 1
            cols = columns(head, dim)
            has_prev, has_next = on & geo.has(f - 1), on & geo.has(f + 1)

            def read(ref):
                return get_stats(ref, pair, side)

            merged = {
                0: merge(read(own), [read(at_prev), read(at_next)], [has_prev, has_next]),
                -1: merge(
                    read(near_prev), [read(own_prev), read(far_prev)],
                    [has_prev, on & geo.has(f - 2)],
                ),
                1: merge(
                    read(near_next), [read(own_next), read(far_next)],
                    [has_next, on & geo.has(f + 2)],
                ),
            }
            sources = {
                0: (q[:, cols], g[:, cols]),
                -1: (prev[slot, 0], prev[slot, 1]),
                1: (following[slot, 0], following[slot, 1]),
            }
            folded = []
            for step in (0, -1, 1):
                where = geo.offsets(offs, f + step)
                keys = geo.keys(k[:, cols], low[0, :, cols], high[0, :, cols], where)
                values = geo.keys(v[:, cols], low[1, :, cols], high[1, :, cols], where)
                query, grad = sources[step]
                s, dp = geo.scores(keys, values, query, grad, where)
                top, inverse, delta = merged[step]
                if step:
                    ok = has_prev if step < 0 else has_next
                    inverse = jnp.where(ok, inverse, jnp.float32(0.0))
                grad_q, grad_k, grad_v = geo.grads(
                    s, dp, keys, query, grad, top, inverse, delta
                )
                folded.append([geo.fold(grad_k, where), geo.fold(grad_v, where)])
                if step == 0:
                    dq_own[slot] = grad_q
                else:
                    out = dq_prev if step < 0 else dq_next
                    out[slot] = grad_q.astype(BF16)
            for j in range(2):
                main, below, above = (
                    folded[0][j][part] + folded[1][j][part] + folded[2][j][part]
                    for part in range(3)
                )
                buf[slot, j] = main.astype(BF16)
                rbuf[slot, 0, j] = below.astype(BF16)
                rbuf[slot, 1, j] = above.astype(BF16)
            for copy in copies(slot):
                copy.start()
        return carry

    def wait(slot, carry):
        for copy in copies(slot):
            copy.wait()
        return carry

    lax.fori_loop(0, n // 2, pair_step, 0)
    lax.fori_loop(0, n, wait, 0)


def last_kernel(n, dim, width, order, *refs):
    if n:
        dq_own, at_prev, at_next, below, above, _, _, _, dq, dk, dv, buf, rows, sems, row_sems = refs
    else:
        below, above, _, _, _, dq, dk, dv, buf, rows, sems, row_sems = refs
    tokens = dk.shape[0]
    places = [
        (ref, start, arrived, j)
        for j, ref in enumerate((dk, dv))
        for start, arrived in ((0, below), (tokens - width, above))
    ]

    def row_copies(back):
        made = []
        for i, (ref, start, _, _) in enumerate(places):
            outer, inner = ref.at[pl.ds(start, width)], rows.at[i]
            if back:
                made.append(pltpu.make_async_copy(inner, outer, row_sems.at[i]))
            else:
                made.append(pltpu.make_async_copy(outer, inner, row_sems.at[i]))
        return made

    for copy in row_copies(False):
        copy.start()

    def copy_of(slot):
        return pltpu.make_async_copy(
            buf.at[slot], dq.at[:, columns(order[slot], dim)], sems.at[slot]
        )

    def add(slot, carry):
        total = dq_own[slot] + at_prev[slot].astype(F32) + at_next[slot].astype(F32)
        buf[slot] = total.astype(BF16)
        copy_of(slot).start()
        return carry

    def wait(slot, carry):
        copy_of(slot).wait()
        return carry

    if n:
        lax.fori_loop(0, n, add, 0)
    for copy in row_copies(False):
        copy.wait()
    for i, (_, _, arrived, j) in enumerate(places):
        rows[i] = (rows[i].astype(F32) + arrived[j].astype(F32)).astype(BF16)
    for copy in row_copies(True):
        copy.start()
    if n:
        lax.fori_loop(0, n, wait, 0)
    for copy in row_copies(True):
        copy.wait()


def call(kernel, ins, outs, out_specs, in_specs, scratch, flops, aliases=None, name=None):
    shapes = [jax.ShapeDtypeStruct(s, d) for s, d in outs]
    moved = sum(x.size * x.dtype.itemsize for x in ins)
    return pl.pallas_call(
        kernel,
        out_shape=shapes,
        in_specs=in_specs,
        out_specs=out_specs,
        scratch_shapes=scratch,
        input_output_aliases=aliases or {},
        cost_estimate=pl.CostEstimate(flops=flops, bytes_accessed=moved, transcendentals=0),
        compiler_params=pltpu.CompilerParams(vmem_limit_bytes=VMEM_LIMIT),
        name=name,
    )(*ins)


def run(n, heads, dim, width, args):
    q, g, k, v, reach, offs = args
    tokens, packed = q.shape
    dma = pltpu.SemaphoreType.DMA
    pairs = n // 2
    rim = ((2, width, packed), BF16)
    whole = ((tokens, packed), BF16)
    tile = (tokens, dim)
    flops = 2 * (tokens + 2 * width) * tokens * dim
    if n:
        order, send, low, high = call(
            functools.partial(pack_kernel, n, heads, dim, width),
            [reach, q, g, k, v],
            [((heads,), jnp.int32), ((n, 2) + tile, BF16), rim, rim],
            [SMEM, VMEM, VMEM, VMEM],
            [SMEM] + [ANY] * 4,
            [dma((n + 2, 2))],
            0,
            name="pack",
        )
        prev, following = shifted(send, "frame", 1), shifted(send, "frame", -1)
    else:
        order = jnp.arange(heads, dtype=jnp.int32)
        low = jnp.stack([k[:width], v[:width]])
        high = jnp.stack([k[tokens - width :], v[tokens - width :]])
    low, high = shifted(high, "row", 1), shifted(low, "row", -1)
    stat = ((max(pairs, 1), 8, tokens), F32)
    rest = max(heads - n, 1)
    own, dq, dk, dv, rim_low, rim_high = call(
        functools.partial(own_kernel, n, heads, dim, width),
        [order, offs, q, g, k, v, low, high],
        [stat, whole, whole, whole, rim, rim],
        [VMEM] + [ANY] * 5,
        [SMEM, SMEM] + [VMEM] * 6,
        [
            pltpu.VMEM((rest, 3) + tile, BF16),
            pltpu.VMEM((rest, 2, 2, width, dim), BF16),
            dma((rest, 5)),
        ],
        flops * (2 * n + 5 * (heads - n)),
        name="own",
    )
    if n:
        own_prev, own_next = shifted(own, "frame", 1), shifted(own, "frame", -1)
        near_prev, near_next = call(
            functools.partial(near_kernel, n, dim, width),
            [order, offs, k, v, low, high, prev, following],
            [stat, stat],
            [VMEM] * 2,
            [SMEM, SMEM] + [VMEM] * 6,
            [],
            flops * 4 * n,
            name="near",
        )
        at_prev, at_next = shifted(near_next, "frame", 1), shifted(near_prev, "frame", -1)
        far_prev, far_next = shifted(near_next, "frame", 2), shifted(near_prev, "frame", -2)
        ins = [
            order, reach, offs, q, g, k, v, low, high, prev, following,
            own, own_prev, own_next, near_prev, near_next, at_prev, at_next, far_prev, far_next,
            dk, dv, rim_low, rim_high,
        ]
        dq_own, dq_prev, dq_next, dk, dv, rim_low, rim_high = call(
            functools.partial(main_kernel, n, dim, width),
            ins,
            [((n,) + tile, F32), ((n,) + tile, BF16), ((n,) + tile, BF16), whole, whole, rim, rim],
            [VMEM] * 3 + [ANY] * 4,
            [SMEM] * 3 + [VMEM] * (len(ins) - 7) + [ANY] * 4,
            [
                pltpu.VMEM((n, 2) + tile, BF16),
                pltpu.VMEM((n, 2, 2, width, dim), BF16),
                dma((n, 4)),
            ],
            flops * 15 * n,
            aliases={20: 3, 21: 4, 22: 5, 23: 6},
            name="main",
        )
        back = [dq_own, shifted(dq_next, "frame", 1), shifted(dq_prev, "frame", -1)]
    else:
        back = []
    below, above = shifted(rim_high, "row", 1), shifted(rim_low, "row", -1)
    ins = [order] + back + [below, above, dq, dk, dv]
    at = len(ins) - 3
    return call(
        functools.partial(last_kernel, n, dim, width),
        ins,
        [whole, whole, whole],
        [ANY] * 3,
        [SMEM] + [VMEM] * (at - 1) + [ANY] * 3,
        [
            pltpu.VMEM((max(n, 1),) + tile, BF16),
            pltpu.VMEM((4, width, packed), BF16),
            dma((max(n, 1),)),
            dma((4,)),
        ],
        0,
        aliases={at: 0, at + 1: 1, at + 2: 2},
        name="last",
    )


def on_device(query_tok, key_tok, value_tok, grad_out, head_reach, tile_offset):
    block = query_tok.shape
    rows_dev, width, packed = block[1:]
    heads = head_reach.shape[0]
    dim = packed // heads
    flat = [x.reshape(rows_dev * width, packed) for x in (query_tok, grad_out, key_tok, value_tok)]
    args = flat + [head_reach, tile_offset]
    sizes = list(range(0, heads + 1, STEP))
    count = jnp.sum(head_reach)
    grads = lax.switch(
        (count + STEP - 1) // STEP,
        [functools.partial(run, n, heads, dim, width) for n in sizes],
        args,
    )
    return tuple(x.reshape(block) for x in grads)


def solution(mesh):
    spec = P("frame", "row", None, None)
    return jax.shard_map(
        on_device,
        mesh=mesh,
        in_specs=(spec, spec, spec, spec, P(), P(None, "row")),
        out_specs=(spec, spec, spec),
        check_vma=False,
    )
```

time: 198 us -> 101 us (0.51)
  waiting for transfers between devices: 107 us -> 16.8 us
  local copies, waits for them, and re-layouts: 31.2 us -> 0.12 us
  Pallas kernels: 0 us -> 30 us
  starting transfers between devices: 27.9 us -> 50.5 us
  other arithmetic: 20.4 us -> 1.29 us
  matrix products: 9.2 us -> 0 us
    ppermute x8 -> x14, waiting for transfers between devices: 107 us -> 16.8 us  [shifted(): return lax.ppermute(block, axis, route)]
    pallas_call x0 -> x5, Pallas kernels: none -> 30 us  [call(): pl.pallas_call(kernel, out_shape=shapes, in_specs=in_specs, out_specs=out...]
    ppermute x8 -> x14, starting transfers between devices: 27.9 us -> 50.5 us  [shifted(): return lax.ppermute(block, axis, route)]
    dot_general x6 -> x0, matrix products: 9.2 us -> none  [the longest x1 2.33 us: tile_attend(): jnp.einsum('bmqk,bkmd->bqmd', dscores, key_w, preferred_element_type=jnp....]
    sub x1 -> x0, other arithmetic: 7.52 us -> none  [tile_attend(): expo = jnp.exp(scores - top)]
    slice x23 -> x0, local copies, waits for them, and re-layouts: 7 us -> none  [the longest x2 1.39 us: make_windows(): padded[:, 4:rows_dev + 4].reshape((frames + 2, tiles, 4, width) + trailing)]
    another operation x7 -> x1, local copies, waits for them, and re-layouts: 6.94 us -> 0.09 us  [the longest x4 3.46 us: on_device(): jnp.stack([key_tok.reshape(1, rows_dev, width, heads, head_dim), value_to...]
    reshape x3 -> x0, local copies, waits for them, and re-layouts: 6.65 us -> none  [the longest x1 2.23 us: on_device(): query_grid = query_tok.reshape(tiles, 4 * width, heads, head_dim)]
  transfers between devices with their start and end apart: 8 -> 14, of which waited for: 5 -> 6; matrix products, arithmetic and copies ran while one was open for 8% -> 0% of each run, Pallas kernels for 0% -> 11%
where the time goes in v1:
time: 101 us
  starting transfers between devices  50.5 us (50%)
  Pallas kernels  30 us (30%)
  waiting for transfers between devices  16.8 us (17%)
  between operations  1.48 us (1%)
  other arithmetic  1.29 us (1%)
    ppermute x14, starting transfers between devices, shifted(): return lax.ppermute(block, axis, route)  50.5 us
    pallas_call x5, Pallas kernels, call(): pl.pallas_call(kernel, out_shape=shapes, in_specs=in_specs, out_specs=out...  30 us
    ppermute x14, waiting for transfers between devices, shifted(): return lax.ppermute(block, axis, route)  16.8 us
  transfers between devices with their start and end apart: 14, of which 6 were waited for; matrix products, arithmetic and copies ran while one was open for 0% of the time, Pallas kernels for 11%

profile of v1, /device:TPU:199, one launch (start us, length us, event | category | flops | bytes accessed | tf_op | source)
XLA Modules:
  0.0 100.9 jit_solution(1519412324479666693)
XLA Ops:
  0.6 1.3 %reduce_sum.9 = s32[]{:T(128)} reduce(s32[20]{0:T(128)} %param.16, s32[]{:T(128)} %constant.16.clone.1), dimensions={0}, to_apply=%region_0.0 | reduce | flops 19 | bytes 88 | tf_op jit(solution)/shard_map/reduce_sum | solution.py:542
  2.6 98.1 %conditional.1 = ((bf16[128,2560]{1,0:T(8,128)(2,1)}, bf16[128,2560]{1,0:T(8,128)(2,1)}, bf16[128,2560]{1,0:T(8,128)(2,1)})) conditional(s32[]{:T(128)} %clamp.3, (bf16[128,2560]{1,0:T(8,128)(2,1)}, bf16[128,2560]{1,0:T(8,128)(2,1)}, s32[32,2]{0,1:T(2,128)}, bf16[128,2560]{1,0:T(8,128)(2,1)}, ...), branch_computations={%region_1.2_spmd, %region_2.3_spmd, %region_3.4_spmd, %region_4.5_... | conditional | flops 2202009600 | bytes 52145920 | solution.py:543
  2.6 0.0 copy-start.30
  2.6 3.1 %pack.7 = (s32[20]{0:T(128)S(1)}, bf16[12,2,128,128]{3,2,1,0:T(8,128)(2,1)S(1)}, bf16[2,16,2560]{2,1,0:T(8,128)(2,1)S(1)}, bf16[2,16,2560]{2,1,0:T(8,128)(2,1)S(1)}) custom-call(s32[20]{0:T(128)} %get-tuple-element.160.reach, bf16[128,2560]{1,0:T(8,128)(2,1)} %get-tuple-element.161.q, bf16[128,2560]{1,0:T(8,128)(2,1)} %get-tuple-element.162.g, ...), custom_call_target="tpu_custom_call" | custom-call | bytes 2621520 | tf_op jit(solution)/shard_map/cond/branch_3_fun/pack/pallas_call | solution.py:421
  5.8 5.4 %collective-permute-start.31 = (bf16[12,2,128,128]{3,2,1,0:T(8,128)(2,1)S(1)}, bf16[12,2,128,128]{3,2,1,0:T(8,128)(2,1)S(1)}, u32[]{:S(2)}, u32[]{:S(2)}) collective-permute-start(bf16[12,2,128,128]{3,2,1,0:T(8,128)(2,1)S(1)} %get-tuple-element.169), channel_id=1, source_target_pairs={{16,0},{32,16},{48,32},{64,48},{80,64},{96,80},{112,96},{128,112},... | collective-permute-start | bytes 2359304 | tf_op jit(solution)/shard_map/cond/branch_3_fun/ppermute | solution.py:22
  11.1 1.9 %collective-permute-start.30 = (bf16[12,2,128,128]{3,2,1,0:T(8,128)(2,1)S(1)}, bf16[12,2,128,128]{3,2,1,0:T(8,128)(2,1)S(1)}, u32[]{:S(2)}, u32[]{:S(2)}) collective-permute-start(bf16[12,2,128,128]{3,2,1,0:T(8,128)(2,1)S(1)} %get-tuple-element.169), channel_id=1, source_target_pairs={{0,16},{16,32},{32,48},{48,64},{64,80},{80,96},{96,112},{112,128},... | collective-permute-start | bytes 2359304 | tf_op jit(solution)/shard_map/cond/branch_3_fun/ppermute | solution.py:22
  13.1 6.1 %collective-permute-start.28 = (bf16[2,16,2560]{2,1,0:T(8,128)(2,1)S(1)}, bf16[2,16,2560]{2,1,0:T(8,128)(2,1)S(1)}, u32[]{:S(2)}, u32[]{:S(2)}) collective-permute-start(bf16[2,16,2560]{2,1,0:T(8,128)(2,1)S(1)} %get-tuple-element.167), channel_id=1, source_target_pairs={{0,1},{1,2},{2,3},{3,4},{4,5},{5,6},{6,7},{7,8},{8,9},{9,10},{10,1... | collective-permute-start | bytes 491528 | tf_op jit(solution)/shard_map/cond/branch_3_fun/ppermute | solution.py:22
  19.1 1.9 %collective-permute-start.29 = (bf16[2,16,2560]{2,1,0:T(8,128)(2,1)S(1)}, bf16[2,16,2560]{2,1,0:T(8,128)(2,1)S(1)}, u32[]{:S(2)}, u32[]{:S(2)}) collective-permute-start(bf16[2,16,2560]{2,1,0:T(8,128)(2,1)S(1)} %get-tuple-element.168), channel_id=1, source_target_pairs={{1,0},{2,1},{3,2},{4,3},{5,4},{6,5},{7,6},{8,7},{9,8},{10,9},{11,1... | collective-permute-start | bytes 491528 | tf_op jit(solution)/shard_map/cond/branch_3_fun/ppermute | solution.py:22
  21.0 0.0 copy-done.30
  21.1 0.1 copy.50.offs
  21.1 0.2 collective-permute-done.28.low
  21.4 5.9 %collective-permute-done.29.high = bf16[2,16,2560]{2,1,0:T(8,128)(2,1)S(1)} collective-permute-done((bf16[2,16,2560]{2,1,0:T(8,128)(2,1)S(1)}, bf16[2,16,2560]{2,1,0:T(8,128)(2,1)S(1)}, u32[]{:S(2)}, u32[]{:S(2)}) %collective-permute-start.29) | collective-permute-done | bytes 163872 | tf_op jit(solution)/shard_map/cond/branch_3_fun/ppermute | solution.py:22
  27.3 0.0 copy-start.3
  27.3 0.0 copy-start.9
  27.3 7.9 %own.9 = (f32[6,8,128]{2,1,0:T(8,128)S(1)}, bf16[128,2560]{1,0:T(8,128)(2,1)}, bf16[128,2560]{1,0:T(8,128)(2,1)}, bf16[128,2560]{1,0:T(8,128)(2,1)}, bf16[2,16,2...) custom-call(s32[20]{0:T(128)S(1)} %get-tuple-element.165.order, s32[32,2]{1,0:T(8,128)S(1)} %copy.50.offs, ...), custom_call_target="tpu_custom_call" | custom-call | flops 335544320 | bytes 2949456 | tf_op jit(solution)/shard_map/cond/branch_3_fun/own/pallas_call | solution.py:421
  35.1 0.0 copy-start.14
  35.2 0.0 copy-start.19
  35.2 0.0 copy-start.24
  35.2 5.9 %collective-permute-start.33 = (f32[6,8,128]{2,1,0:T(8,128)S(1)}, f32[6,8,128]{2,1,0:T(8,128)S(1)}, u32[]{:S(2)}, u32[]{:S(2)}) collective-permute-start(f32[6,8,128]{2,1,0:T(8,128)S(1)} %get-tuple-element.170.own), channel_id=1, source_target_pairs={{16,0},{32,16},{48,32},{64,48},{80,64},{96,80},{112,96},{128,112},... | collective-permute-start | bytes 73736 | tf_op jit(solution)/shard_map/cond/branch_3_fun/ppermute | solution.py:22
  41.1 1.9 %collective-permute-start.32 = (f32[6,8,128]{2,1,0:T(8,128)S(1)}, f32[6,8,128]{2,1,0:T(8,128)S(1)}, u32[]{:S(2)}, u32[]{:S(2)}) collective-permute-start(f32[6,8,128]{2,1,0:T(8,128)S(1)} %get-tuple-element.170.own), channel_id=1, source_target_pairs={{0,16},{16,32},{32,48},{48,64},{64,80},{80,96},{96,112},{112,128},... | collective-permute-start | bytes 73736 | tf_op jit(solution)/shard_map/cond/branch_3_fun/ppermute | solution.py:22
  43.0 0.0 collective-permute-done.31.following
  43.0 0.0 collective-permute-done.30.prev
  43.0 0.0 copy-done.3
  43.0 0.0 copy-done.9
  43.0 2.9 %near.7 = (f32[6,8,128]{2,1,0:T(8,128)S(1)}, f32[6,8,128]{2,1,0:T(8,128)S(1)}) custom-call(s32[20]{0:T(128)S(1)} %get-tuple-element.165.order, s32[32,2]{1,0:T(8,128)S(1)} %copy.50.offs, bf16[128,2560]{1,0:T(8,128)(2,1)S(1)} %copy-done.3, bf16[128,2560]{1,0:T(8,128)(2,1)S(1)} %copy-done.9, bf16[2,16,2560]{2,1,0:T(8,128)(2,1)S(1)} %collective-permute-done.28.low, ...), custom_call_target="tpu_custom_call" | custom-call | flops 251658240 | bytes 3211600 | tf_op jit(solution)/shard_map/cond/branch_3_fun/near/pallas_call | solution.py:421
  45.9 3.1 %collective-permute-start.37 = (f32[6,8,128]{2,1,0:T(8,128)S(1)}, f32[6,8,128]{2,1,0:T(8,128)S(1)}, u32[]{:S(2)}, u32[]{:S(2)}) collective-permute-start(f32[6,8,128]{2,1,0:T(8,128)S(1)} %get-tuple-element.171.near_prev), channel_id=1, source_target_pairs={{32,0},{48,16},{64,32},{80,48},{96,64},{112,80},{128,96},{144,112}... | collective-permute-start | bytes 73736 | tf_op jit(solution)/shard_map/cond/branch_3_fun/ppermute | solution.py:22
  49.0 4.3 %collective-permute-start.35 = (f32[6,8,128]{2,1,0:T(8,128)S(1)}, f32[6,8,128]{2,1,0:T(8,128)S(1)}, u32[]{:S(2)}, u32[]{:S(2)}) collective-permute-start(f32[6,8,128]{2,1,0:T(8,128)S(1)} %get-tuple-element.171.near_prev), channel_id=1, source_target_pairs={{16,0},{32,16},{48,32},{64,48},{80,64},{96,80},{112,96},{128,112},... | collective-permute-start | bytes 73736 | tf_op jit(solution)/shard_map/cond/branch_3_fun/ppermute | solution.py:22
  53.3 4.3 %collective-permute-start.36 = (f32[6,8,128]{2,1,0:T(8,128)S(1)}, f32[6,8,128]{2,1,0:T(8,128)S(1)}, u32[]{:S(2)}, u32[]{:S(2)}) collective-permute-start(f32[6,8,128]{2,1,0:T(8,128)S(1)} %get-tuple-element.172.near_next), channel_id=1, source_target_pairs={{0,32},{16,48},{32,64},{48,80},{64,96},{80,112},{96,128},{112,144}... | collective-permute-start | bytes 73736 | tf_op jit(solution)/shard_map/cond/branch_3_fun/ppermute | solution.py:22
  57.6 0.0 collective-permute-done.33.own_next
  57.6 1.9 %collective-permute-start.34 = (f32[6,8,128]{2,1,0:T(8,128)S(1)}, f32[6,8,128]{2,1,0:T(8,128)S(1)}, u32[]{:S(2)}, u32[]{:S(2)}) collective-permute-start(f32[6,8,128]{2,1,0:T(8,128)S(1)} %get-tuple-element.172.near_next), channel_id=1, source_target_pairs={{0,16},{16,32},{32,48},{48,64},{64,80},{80,96},{96,112},{112,128},... | collective-permute-start | bytes 73736 | tf_op jit(solution)/shard_map/cond/branch_3_fun/ppermute | solution.py:22
  59.6 0.0 collective-permute-done.32.own_prev
  59.6 0.0 collective-permute-done.37.far_next
  59.6 0.0 collective-permute-done.35.at_next
  59.6 1.6 %collective-permute-done.36.far_prev = f32[6,8,128]{2,1,0:T(8,128)S(1)} collective-permute-done((f32[6,8,128]{2,1,0:T(8,128)S(1)}, f32[6,8,128]{2,1,0:T(8,128)S(1)}, u32[]{:S(2)}, u32[]{:S(2)}) %collective-permute-start.36) | collective-permute-done | bytes 24608 | tf_op jit(solution)/shard_map/cond/branch_3_fun/ppermute | solution.py:22
  61.1 3.2 %collective-permute-done.34.at_prev = f32[6,8,128]{2,1,0:T(8,128)S(1)} collective-permute-done((f32[6,8,128]{2,1,0:T(8,128)S(1)}, f32[6,8,128]{2,1,0:T(8,128)S(1)}, u32[]{:S(2)}, u32[]{:S(2)}) %collective-permute-start.34) | collective-permute-done | bytes 24608 | tf_op jit(solution)/shard_map/cond/branch_3_fun/ppermute | solution.py:22
  64.3 0.0 copy-done.14
  64.3 0.0 copy-done.19
  64.3 0.0 copy-done.24
  64.3 13.5 %main.7 = (f32[12,128,128]{2,1,0:T(8,128)S(1)}, bf16[12,128,128]{2,1,0:T(8,128)(2,1)S(1)}, bf16[12,128,128]{2,1,0:T(8,128)(2,1)S(1)}, bf16[128,2560]{1,0:T(8,128...) custom-call(s32[20]{0:T(128)S(1)} %get-tuple-element.165.order, ...), custom_call_target="tpu_custom_call", output_to_operand_aliasing={{3}: (20, {}), {4}: (21, {}), {5}: (22, {}), {6}: (23, {})} | custom-call | flops 943718400 | bytes 6381984 | tf_op jit(solution)/shard_map/cond/branch_3_fun/main/pallas_call | solution.py:421
  77.8 1.9 %collective-permute-start.38 = (bf16[12,128,128]{2,1,0:T(8,128)(2,1)S(1)}, bf16[12,128,128]{2,1,0:T(8,128)(2,1)S(1)}, u32[]{:S(2)}, u32[]{:S(2)}) collective-permute-start(bf16[12,128,128]{2,1,0:T(8,128)(2,1)S(1)} %get-tuple-element.178), channel_id=1, source_target_pairs={{0,16},{16,32},{32,48},{48,64},{64,80},{80,96},{96,112},{112,128},... | collective-permute-start | bytes 1179656 | tf_op jit(solution)/shard_map/cond/branch_3_fun/ppermute | solution.py:22
  79.7 5.5 %collective-permute-start.39 = (bf16[12,128,128]{2,1,0:T(8,128)(2,1)S(1)}, bf16[12,128,128]{2,1,0:T(8,128)(2,1)S(1)}, u32[]{:S(2)}, u32[]{:S(2)}) collective-permute-start(bf16[12,128,128]{2,1,0:T(8,128)(2,1)S(1)} %get-tuple-element.179), channel_id=1, source_target_pairs={{16,0},{32,16},{48,32},{64,48},{80,64},{96,80},{112,96},{128,112},... | collective-permute-start | bytes 1179656 | tf_op jit(solution)/shard_map/cond/branch_3_fun/ppermute | solution.py:22
  85.2 4.6 %collective-permute-start.40 = (bf16[2,16,2560]{2,1,0:T(8,128)(2,1)S(1)}, bf16[2,16,2560]{2,1,0:T(8,128)(2,1)S(1)}, u32[]{:S(2)}, u32[]{:S(2)}) collective-permute-start(bf16[2,16,2560]{2,1,0:T(8,128)(2,1)S(1)} %get-tuple-element.180), channel_id=1, source_target_pairs={{0,1},{1,2},{2,3},{3,4},{4,5},{5,6},{6,7},{7,8},{8,9},{9,10},{10,1... | collective-permute-start | bytes 491528 | tf_op jit(solution)/shard_map/cond/branch_3_fun/ppermute | solution.py:22
  89.8 1.9 %collective-permute-start.41 = (bf16[2,16,2560]{2,1,0:T(8,128)(2,1)S(1)}, bf16[2,16,2560]{2,1,0:T(8,128)(2,1)S(1)}, u32[]{:S(2)}, u32[]{:S(2)}) collective-permute-start(bf16[2,16,2560]{2,1,0:T(8,128)(2,1)S(1)} %get-tuple-element.181), channel_id=1, source_target_pairs={{1,0},{2,1},{3,2},{4,3},{5,4},{6,5},{7,6},{8,7},{9,8},{10,9},{11,1... | collective-permute-start | bytes 491528 | tf_op jit(solution)/shard_map/cond/branch_3_fun/ppermute | solution.py:22
  91.7 0.3 collective-permute-done.40.refs_3_
  92.0 5.6 %collective-permute-done.41.refs_4_ = bf16[2,16,2560]{2,1,0:T(8,128)(2,1)S(1)} collective-permute-done((bf16[2,16,2560]{2,1,0:T(8,128)(2,1)S(1)}, bf16[2,16,2560]{2,1,0:T(8,128)(2,1)S(1)}, u32[]{:S(2)}, u32[]{:S(2)}) %collective-permute-start.41) | collective-permute-done | bytes 163872 | tf_op jit(solution)/shard_map/cond/branch_3_fun/ppermute | solution.py:22
  97.6 0.0 collective-permute-done.38.refs_1_
  97.6 0.0 collective-permute-done.39.refs_2_
  97.6 2.6 %last.9 = (bf16[128,2560]{1,0:T(8,128)(2,1)}, bf16[128,2560]{1,0:T(8,128)(2,1)}, bf16[128,2560]{1,0:T(8,128)(2,1)}) custom-call(s32[20]{0:T(128)S(1)} %get-tuple-element.165.order, f32[12,128,128]{2,1,0:T(8,128)S(1)} %get-tuple-element.177.refs_0_, ...), custom_call_target="tpu_custom_call", output_to_operand_aliasing={{0}: (6, {}), {1}: (7, {}), {2}: (8, {})} | custom-call | bytes 3866704 | tf_op jit(solution)/shard_map/cond/branch_3_fun/last/pallas_call | solution.py:421
Async XLA Ops:
  2.6 18.4 %copy-start.30 = (s32[32,2]{0,1:T(2,128)S(1)}, s32[32,2]{0,1:T(2,128)}, u32[]{:S(2)}) copy-start(s32[32,2]{0,1:T(2,128)} %get-tuple-element.273) | copy-start | bytes 772 | tf_op jit(solution)/shard_map/cond
  5.8 37.2 %collective-permute-start.31 = (bf16[12,2,128,128]{3,2,1,0:T(8,128)(2,1)S(1)}, bf16[12,2,128,128]{3,2,1,0:T(8,128)(2,1)S(1)}, u32[]{:S(2)}, u32[]{:S(2)}) collective-permute-start(bf16[12,2,128,128]{3,2,1,0:T(8,128)(2,1)S(1)} %get-tuple-element.169), channel_id=1, source_target_pairs={{16,0},{32,16},{48,32},{64,48},{80,64},{96,80},{112,96},{128,112},... | collective-permute-start | bytes 2359304 | tf_op jit(solution)/shard_map/cond/branch_3_fun/ppermute | solution.py:22
  11.1 31.9 %collective-permute-start.30 = (bf16[12,2,128,128]{3,2,1,0:T(8,128)(2,1)S(1)}, bf16[12,2,128,128]{3,2,1,0:T(8,128)(2,1)S(1)}, u32[]{:S(2)}, u32[]{:S(2)}) collective-permute-start(bf16[12,2,128,128]{3,2,1,0:T(8,128)(2,1)S(1)} %get-tuple-element.169), channel_id=1, source_target_pairs={{0,16},{16,32},{32,48},{48,64},{64,80},{80,96},{96,112},{112,128},... | collective-permute-start | bytes 2359304 | tf_op jit(solution)/shard_map/cond/branch_3_fun/ppermute | solution.py:22
  13.1 8.3 %collective-permute-start.28 = (bf16[2,16,2560]{2,1,0:T(8,128)(2,1)S(1)}, bf16[2,16,2560]{2,1,0:T(8,128)(2,1)S(1)}, u32[]{:S(2)}, u32[]{:S(2)}) collective-permute-start(bf16[2,16,2560]{2,1,0:T(8,128)(2,1)S(1)} %get-tuple-element.167), channel_id=1, source_target_pairs={{0,1},{1,2},{2,3},{3,4},{4,5},{5,6},{6,7},{7,8},{8,9},{9,10},{10,1... | collective-permute-start | bytes 491528 | tf_op jit(solution)/shard_map/cond/branch_3_fun/ppermute | solution.py:22
  19.1 8.1 %collective-permute-start.29 = (bf16[2,16,2560]{2,1,0:T(8,128)(2,1)S(1)}, bf16[2,16,2560]{2,1,0:T(8,128)(2,1)S(1)}, u32[]{:S(2)}, u32[]{:S(2)}) collective-permute-start(bf16[2,16,2560]{2,1,0:T(8,128)(2,1)S(1)} %get-tuple-element.168), channel_id=1, source_target_pairs={{1,0},{2,1},{3,2},{4,3},{5,4},{6,5},{7,6},{8,7},{9,8},{10,9},{11,1... | collective-permute-start | bytes 491528 | tf_op jit(solution)/shard_map/cond/branch_3_fun/ppermute | solution.py:22
  27.3 15.8 %copy-start.3 = (bf16[128,2560]{1,0:T(8,128)(2,1)S(1)}, bf16[128,2560]{1,0:T(8,128)(2,1)}, u32[]{:S(2)}) copy-start(bf16[128,2560]{1,0:T(8,128)(2,1)} %get-tuple-element.163.k) | copy-start | bytes 1966084 | tf_op jit(solution)/shard_map/cond
  27.3 15.8 %copy-start.9 = (bf16[128,2560]{1,0:T(8,128)(2,1)S(1)}, bf16[128,2560]{1,0:T(8,128)(2,1)}, u32[]{:S(2)}) copy-start(bf16[128,2560]{1,0:T(8,128)(2,1)} %get-tuple-element.164.v) | copy-start | bytes 1966084 | tf_op jit(solution)/shard_map/cond
  35.1 29.2 %copy-start.14 = (bf16[128,2560]{1,0:T(8,128)(2,1)S(1)}, bf16[128,2560]{1,0:T(8,128)(2,1)}, u32[]{:S(2)}) copy-start(bf16[128,2560]{1,0:T(8,128)(2,1)} %get-tuple-element.161.q) | copy-start | bytes 1966084 | tf_op jit(solution)/shard_map/cond
  35.2 29.1 %copy-start.19 = (bf16[128,2560]{1,0:T(8,128)(2,1)S(1)}, bf16[128,2560]{1,0:T(8,128)(2,1)}, u32[]{:S(2)}) copy-start(bf16[128,2560]{1,0:T(8,128)(2,1)} %get-tuple-element.162.g) | copy-start | bytes 1966084 | tf_op jit(solution)/shard_map/cond
  35.2 29.1 %copy-start.24 = (s32[20]{0:T(128)S(1)}, s32[20]{0:T(128)}, u32[]{:S(2)}) copy-start(s32[20]{0:T(128)} %get-tuple-element.160.reach) | copy-start | bytes 244 | tf_op jit(solution)/shard_map/cond
  35.2 22.4 %collective-permute-start.33 = (f32[6,8,128]{2,1,0:T(8,128)S(1)}, f32[6,8,128]{2,1,0:T(8,128)S(1)}, u32[]{:S(2)}, u32[]{:S(2)}) collective-permute-start(f32[6,8,128]{2,1,0:T(8,128)S(1)} %get-tuple-element.170.own), channel_id=1, source_target_pairs={{16,0},{32,16},{48,32},{64,48},{80,64},{96,80},{112,96},{128,112},... | collective-permute-start | bytes 73736 | tf_op jit(solution)/shard_map/cond/branch_3_fun/ppermute | solution.py:22
  41.1 18.5 %collective-permute-start.32 = (f32[6,8,128]{2,1,0:T(8,128)S(1)}, f32[6,8,128]{2,1,0:T(8,128)S(1)}, u32[]{:S(2)}, u32[]{:S(2)}) collective-permute-start(f32[6,8,128]{2,1,0:T(8,128)S(1)} %get-tuple-element.170.own), channel_id=1, source_target_pairs={{0,16},{16,32},{32,48},{48,64},{64,80},{80,96},{96,112},{112,128},... | collective-permute-start | bytes 73736 | tf_op jit(solution)/shard_map/cond/branch_3_fun/ppermute | solution.py:22
  45.9 13.6 %collective-permute-start.37 = (f32[6,8,128]{2,1,0:T(8,128)S(1)}, f32[6,8,128]{2,1,0:T(8,128)S(1)}, u32[]{:S(2)}, u32[]{:S(2)}) collective-permute-start(f32[6,8,128]{2,1,0:T(8,128)S(1)} %get-tuple-element.171.near_prev), channel_id=1, source_target_pairs={{32,0},{48,16},{64,32},{80,48},{96,64},{112,80},{128,96},{144,112}... | collective-permute-start | bytes 73736 | tf_op jit(solution)/shard_map/cond/branch_3_fun/ppermute | solution.py:22
  49.0 10.5 %collective-permute-start.35 = (f32[6,8,128]{2,1,0:T(8,128)S(1)}, f32[6,8,128]{2,1,0:T(8,128)S(1)}, u32[]{:S(2)}, u32[]{:S(2)}) collective-permute-start(f32[6,8,128]{2,1,0:T(8,128)S(1)} %get-tuple-element.171.near_prev), channel_id=1, source_target_pairs={{16,0},{32,16},{48,32},{64,48},{80,64},{96,80},{112,96},{128,112},... | collective-permute-start | bytes 73736 | tf_op jit(solution)/shard_map/cond/branch_3_fun/ppermute | solution.py:22
  53.3 7.8 %collective-permute-start.36 = (f32[6,8,128]{2,1,0:T(8,128)S(1)}, f32[6,8,128]{2,1,0:T(8,128)S(1)}, u32[]{:S(2)}, u32[]{:S(2)}) collective-permute-start(f32[6,8,128]{2,1,0:T(8,128)S(1)} %get-tuple-element.172.near_next), channel_id=1, source_target_pairs={{0,32},{16,48},{32,64},{48,80},{64,96},{80,112},{96,128},{112,144}... | collective-permute-start | bytes 73736 | tf_op jit(solution)/shard_map/cond/branch_3_fun/ppermute | solution.py:22
  57.6 6.7 %collective-permute-start.34 = (f32[6,8,128]{2,1,0:T(8,128)S(1)}, f32[6,8,128]{2,1,0:T(8,128)S(1)}, u32[]{:S(2)}, u32[]{:S(2)}) collective-permute-start(f32[6,8,128]{2,1,0:T(8,128)S(1)} %get-tuple-element.172.near_next), channel_id=1, source_target_pairs={{0,16},{16,32},{32,48},{48,64},{64,80},{80,96},{96,112},{112,128},... | collective-permute-start | bytes 73736 | tf_op jit(solution)/shard_map/cond/branch_3_fun/ppermute | solution.py:22
  77.8 19.8 %collective-permute-start.38 = (bf16[12,128,128]{2,1,0:T(8,128)(2,1)S(1)}, bf16[12,128,128]{2,1,0:T(8,128)(2,1)S(1)}, u32[]{:S(2)}, u32[]{:S(2)}) collective-permute-start(bf16[12,128,128]{2,1,0:T(8,128)(2,1)S(1)} %get-tuple-element.178), channel_id=1, source_target_pairs={{0,16},{16,32},{32,48},{48,64},{64,80},{80,96},{96,112},{112,128},... | collective-permute-start | bytes 1179656 | tf_op jit(solution)/shard_map/cond/branch_3_fun/ppermute | solution.py:22
  79.7 17.9 %collective-permute-start.39 = (bf16[12,128,128]{2,1,0:T(8,128)(2,1)S(1)}, bf16[12,128,128]{2,1,0:T(8,128)(2,1)S(1)}, u32[]{:S(2)}, u32[]{:S(2)}) collective-permute-start(bf16[12,128,128]{2,1,0:T(8,128)(2,1)S(1)} %get-tuple-element.179), channel_id=1, source_target_pairs={{16,0},{32,16},{48,32},{64,48},{80,64},{96,80},{112,96},{128,112},... | collective-permute-start | bytes 1179656 | tf_op jit(solution)/shard_map/cond/branch_3_fun/ppermute | solution.py:22
  85.2 6.8 %collective-permute-start.40 = (bf16[2,16,2560]{2,1,0:T(8,128)(2,1)S(1)}, bf16[2,16,2560]{2,1,0:T(8,128)(2,1)S(1)}, u32[]{:S(2)}, u32[]{:S(2)}) collective-permute-start(bf16[2,16,2560]{2,1,0:T(8,128)(2,1)S(1)} %get-tuple-element.180), channel_id=1, source_target_pairs={{0,1},{1,2},{2,3},{3,4},{4,5},{5,6},{6,7},{7,8},{8,9},{9,10},{10,1... | collective-permute-start | bytes 491528 | tf_op jit(solution)/shard_map/cond/branch_3_fun/ppermute | solution.py:22
  89.8 7.8 %collective-permute-start.41 = (bf16[2,16,2560]{2,1,0:T(8,128)(2,1)S(1)}, bf16[2,16,2560]{2,1,0:T(8,128)(2,1)S(1)}, u32[]{:S(2)}, u32[]{:S(2)}) collective-permute-start(bf16[2,16,2560]{2,1,0:T(8,128)(2,1)S(1)} %get-tuple-element.181), channel_id=1, source_target_pairs={{1,0},{2,1},{3,2},{4,3},{5,4},{6,5},{7,6},{8,7},{9,8},{10,9},{11,1... | collective-permute-start | bytes 491528 | tf_op jit(solution)/shard_map/cond/branch_3_fun/ppermute | solution.py:22

commit v2 on v1

v2 whole, which is shorter than its diff:
```python
import functools
import math

import jax
import jax.numpy as jnp
from jax import lax
from jax.experimental import pallas as pl
from jax.experimental.pallas import tpu as pltpu
from jax.sharding import PartitionSpec as P

STEP = 4
VMEM_LIMIT = 24 << 20
F32, BF16 = jnp.float32, jnp.bfloat16
SMEM = pl.BlockSpec(memory_space=pltpu.SMEM)
VMEM = pl.BlockSpec(memory_space=pltpu.VMEM)


def shifted(block, axis, distance):
    devices = range(lax.axis_size(axis))
    route = [(i - distance, i) for i in devices if i - distance in devices]
    return lax.ppermute(block, axis, route)


def swapped(block, axis, first):
    count = lax.axis_size(axis)
    pairs = [(i, i + 1) for i in range(first, count - 1, 2)]
    return lax.ppermute(block, axis, pairs + [(b, a) for a, b in pairs])


def columns(head, dim):
    return pl.ds(pl.multiple_of(head * dim, dim), dim)


def dot_nt(a, b):
    return lax.dot_general(a, b, (((1,), (1,)), ((), ())), preferred_element_type=F32)


def dot_nn(a, b):
    return lax.dot_general(a, b, (((1,), (0,)), ((), ())), preferred_element_type=F32)


def dot_tn(a, b):
    return lax.dot_general(a, b, (((0,), (0,)), ((), ())), preferred_element_type=F32)


class Geometry:
    def __init__(self, tokens, width, dim):
        self.tokens, self.width, self.dim = tokens, width, dim
        self.half = tokens // 2
        self.scale = 1.0 / math.sqrt(dim)
        self.frames = lax.axis_size("frame")
        self.frame = lax.axis_index("frame")
        self.row = lax.axis_index("row")
        self.rows = lax.axis_size("row")
        self.even = lax.rem(self.row, 2) == 0
        self.low_lanes = lax.broadcasted_iota(jnp.int32, (1, tokens), 1) < self.half

    def has(self, frame):
        return (frame >= 0) & (frame < self.frames)

    def offsets(self, offs_ref, frame):
        frame = jnp.clip(frame, 0, self.frames - 1)
        first, second = offs_ref[frame, 0], offs_ref[frame, 1]
        lost0 = (first == -1) & (self.row == 0)
        lost1 = (second == 0) & (self.row == self.rows - 1)
        fine, gone = jnp.float32(0.0), jnp.float32(-1e30)
        penalty = jnp.where(
            self.low_lanes, jnp.where(lost0, gone, fine), jnp.where(lost1, gone, fine)
        )
        return first == -1, second == -1, penalty

    def rims(self, near, far):
        return jnp.where(self.even, far, near), jnp.where(self.even, near, far)

    def keys(self, main, low, high, offs):
        half, width = self.half, self.width
        edge0 = jnp.where(offs[0], low, main[half : half + width])
        edge1 = jnp.where(offs[1], main[half - width : half], high)
        return jnp.concatenate([main, edge0, edge1], axis=0)

    def keys_of(self, extended, offs):
        width, end = self.width, self.width + self.tokens
        return self.keys(extended[width:end], extended[:width], extended[end:], offs)

    def by_tile(self, product):
        half, width, tokens = self.half, self.width, self.tokens
        own = jnp.where(self.low_lanes, product[:half], product[half:tokens])
        edge = jnp.where(
            self.low_lanes, product[tokens : tokens + width], product[tokens + width :]
        )
        return own, edge

    def scores(self, keys, values, query, grad, offs):
        own, edge = self.by_tile(dot_nt(keys, query))
        s = jnp.concatenate([own * self.scale, edge * self.scale + offs[2]], axis=0)
        dp = jnp.concatenate(self.by_tile(dot_nt(values, grad)), axis=0)
        return s, dp

    def spread(self, terms):
        half = self.half
        own, edge = terms[:half], terms[half:]
        zero_own, zero_edge = jnp.zeros_like(own), jnp.zeros_like(edge)
        low = self.low_lanes
        return jnp.concatenate(
            [
                jnp.where(low, own, zero_own).astype(BF16),
                jnp.where(low, zero_own, own).astype(BF16),
                jnp.where(low, edge, zero_edge).astype(BF16),
                jnp.where(low, zero_edge, edge).astype(BF16),
            ],
            axis=0,
        )

    def weigh(self, s, dp, top, inverse, delta):
        p = jnp.exp(s - top) * inverse
        ds = p * (dp - delta) * self.scale
        return self.spread(p), self.spread(ds)

    def fold(self, term, offs):
        half, width, tokens = self.half, self.width, self.tokens
        edge0, edge1 = term[tokens : tokens + width], term[tokens + width :]
        none = jnp.zeros_like(edge0)
        return jnp.concatenate(
            [
                jnp.where(offs[0], edge0, none),
                term[: half - width],
                term[half - width : half] + jnp.where(offs[1], edge1, none),
                term[half : half + width] + jnp.where(offs[0], none, edge0),
                term[half + width : tokens],
                jnp.where(offs[1], none, edge1),
            ],
            axis=0,
        )


def stats_of(s, dp):
    top = jnp.max(s, axis=0, keepdims=True)
    expo = jnp.exp(s - top)
    return top, jnp.sum(expo, axis=0, keepdims=True), jnp.sum(expo * dp, axis=0, keepdims=True)


def put_stats(ref, pair, side, stats):
    for j, row in enumerate(stats):
        ref[pair, pl.ds(4 * side + j, 1), :] = row


def get_stats(ref, pair, side):
    return [ref[pair, pl.ds(4 * side + j, 1), :] for j in range(3)]


def merge(first, others, valid):
    low = jnp.float32(-1e30)
    tops = [first[0]] + [jnp.where(ok, o[0], low) for o, ok in zip(others, valid)]
    top = functools.reduce(jnp.maximum, tops)
    factor = jnp.exp(first[0] - top)
    total, weighted = first[1] * factor, first[2] * factor
    for o, ok, t in zip(others, valid, tops[1:]):
        factor = jnp.where(ok, jnp.exp(t - top), jnp.float32(0.0))
        total, weighted = total + o[1] * factor, weighted + o[2] * factor
    inverse = 1.0 / total
    return top, inverse, weighted * inverse


def edge_kernel(heads, width, reach, k, v, order, near, far):
    tokens = k.shape[0]
    even = lax.rem(lax.axis_index("row"), 2) == 0
    for j, ref in enumerate((k, v)):
        first, last = ref[:width], ref[tokens - width :]
        near[j] = jnp.where(even, last, first)
        far[j] = jnp.where(even, first, last)
    count = lax.fori_loop(0, heads, lambda h, c: c + reach[h], 0)

    def place(h, carry):
        on, off = carry
        hit = reach[h] == 1
        order[jnp.where(hit, on, off)] = h
        return jnp.where(hit, on + 1, on), jnp.where(hit, off, off + 1)

    lax.fori_loop(0, heads, place, (0, count))


def pack_kernel(n, dim, order, q, g, send):
    for slot in range(n):
        cols = columns(order[slot], dim)
        send[slot, 0] = q[:, cols]
        send[slot, 1] = g[:, cols]


def extend_kernel(n, dim, width, order, k, v, near, far, send):
    tokens = k.shape[0]
    geo = Geometry(tokens, width, dim)
    for slot in range(n):
        cols = columns(order[slot], dim)
        for j, ref in enumerate((k, v)):
            low, high = geo.rims(near[j, :, cols], far[j, :, cols])
            send[slot, j, :width] = low
            send[slot, j, width : width + tokens] = ref[:, cols]
            send[slot, j, width + tokens :] = high


def own_kernel(n, heads, dim, width, order, offs, q, g, k, v, near, far, grads, rims):
    tokens = q.shape[0]
    geo = Geometry(tokens, width, dim)
    where = geo.offsets(offs, geo.frame)

    def finish(pair, carry):
        for side in range(2):
            i = 2 * pair + side
            cols = columns(order[n + i], dim)
            low, high = geo.rims(near[0, :, cols], far[0, :, cols])
            keys = geo.keys(k[:, cols], low, high, where)
            low, high = geo.rims(near[1, :, cols], far[1, :, cols])
            values = geo.keys(v[:, cols], low, high, where)
            query, grad = q[:, cols], g[:, cols]
            s, dp = geo.scores(keys, values, query, grad, where)
            top, total, weighted = stats_of(s, dp)
            inverse = 1.0 / total
            weights, dscores = geo.weigh(s, dp, top, inverse, weighted * inverse)
            grads[i, 0] = dot_tn(dscores, keys).astype(BF16)
            for j, term in enumerate((dot_nn(dscores, query), dot_nn(weights, grad))):
                folded = geo.fold(term, where)
                grads[i, 1 + j] = folded[width : width + tokens].astype(BF16)
                rims[i, 0, j] = folded[:width].astype(BF16)
                rims[i, 1, j] = folded[width + tokens :].astype(BF16)
        return carry

    lax.fori_loop(0, (heads - n) // 2, finish, 0)


def query_kernel(n, dim, width, order, reach, offs, own_q, own, prev, following, stats, s_out, dp_out):
    geo = Geometry(own_q.shape[2], width, dim)
    where = geo.offsets(offs, geo.frame)
    has_prev, has_next = geo.has(geo.frame - 1), geo.has(geo.frame + 1)

    def pair_step(pair, carry):
        for side in range(2):
            slot = 2 * pair + side
            on = reach[order[slot]] == 1
            parts = []
            for i, block in enumerate((own, prev, following)):
                keys = geo.keys_of(block[slot, 0], where)
                values = geo.keys_of(block[slot, 1], where)
                s, dp = geo.scores(keys, values, own_q[slot, 0], own_q[slot, 1], where)
                s_out[slot, i] = s
                dp_out[slot, i] = dp
                parts.append(stats_of(s, dp))
            put_stats(stats, pair, side, merge(parts[0], parts[1:], [on & has_prev, on & has_next]))
        return carry

    lax.fori_loop(0, n // 2, pair_step, 0)


def finish_kernel(
    n, dim, width, order, reach, offs, own_q, own, prev, following, stats, s_in, dp_in, acc, dq
):
    geo = Geometry(own_q.shape[2], width, dim)
    where = geo.offsets(offs, geo.frame)
    has_prev, has_next = geo.has(geo.frame - 1), geo.has(geo.frame + 1)

    def pair_step(pair, carry):
        for side in range(2):
            slot = 2 * pair + side
            on = reach[order[slot]] == 1
            top, inverse, delta = get_stats(stats, pair, side)
            total = None
            for i, (block, ok) in enumerate(
                ((own, None), (prev, on & has_prev), (following, on & has_next))
            ):
                keys = geo.keys_of(block[slot, 0], where)
                part = inverse if ok is None else jnp.where(ok, inverse, jnp.float32(0.0))
                s = s_in[slot, i] if ok is None else jnp.minimum(s_in[slot, i], top)
                weights, dscores = geo.weigh(s, dp_in[slot, i], top, part, delta)
                term = dot_tn(dscores, keys)
                total = term if total is None else total + term
                if ok is None:
                    acc[slot, 0] = geo.fold(dot_nn(dscores, own_q[slot, 0]), where)
                    acc[slot, 1] = geo.fold(dot_nn(weights, own_q[slot, 1]), where)
            dq[slot] = total.astype(BF16)
        return carry

    lax.fori_loop(0, n // 2, pair_step, 0)


def key_kernel(
    n, dim, width, order, reach, offs, own, q_prev, q_next, st_prev, st_next, acc, *refs
):
    tokens = q_prev.shape[2]
    geo = Geometry(tokens, width, dim)
    others, (grads, rim_low, rim_high) = refs[:-3], refs[-3:]

    def pair_step(pair, carry):
        for side in range(2):
            slot = 2 * pair + side
            head = order[slot]
            on = reach[head] == 1
            total = [acc[slot, 0], acc[slot, 1]]
            for step, queries, stats in ((-1, q_prev, st_prev), (1, q_next, st_next)):
                where = geo.offsets(offs, geo.frame + step)
                keys = geo.keys_of(own[slot, 0], where)
                values = geo.keys_of(own[slot, 1], where)
                query, grad = queries[slot, 0], queries[slot, 1]
                s, dp = geo.scores(keys, values, query, grad, where)
                top, inverse, delta = get_stats(stats, pair, side)
                ok = on & geo.has(geo.frame + step)
                inverse = jnp.where(ok, inverse, jnp.float32(0.0))
                weights, dscores = geo.weigh(jnp.minimum(s, top), dp, top, inverse, delta)
                total[0] = total[0] + geo.fold(dot_nn(dscores, query), where)
                total[1] = total[1] + geo.fold(dot_nn(weights, grad), where)
            cols = columns(head, dim)
            for j in range(2):
                grads[slot, j] = total[j][width : width + tokens].astype(BF16)
                rim_low[j, :, cols] = total[j][:width].astype(BF16)
                rim_high[j, :, cols] = total[j][width + tokens :].astype(BF16)
        return carry

    lax.fori_loop(0, n // 2, pair_step, 0)
    if others:
        spread_rims(n, order, others[0], rim_low, rim_high, dim)


def spread_rims(n, order, rims, rim_low, rim_high, dim):
    for i in range(rims.shape[0]):
        cols = columns(order[n + i], dim)
        for j in range(2):
            rim_low[j, :, cols] = rims[i, 0, j]
            rim_high[j, :, cols] = rims[i, 1, j]


def rim_kernel(dim, order, rims, rim_low, rim_high):
    spread_rims(0, order, rims, rim_low, rim_high, dim)


def query_out_kernel(n, dim, order, *refs):
    parts, out = refs[:-1], refs[-1]
    for slot in range(n):
        out[:, columns(order[slot], dim)] = parts[0][slot]
    if len(parts) > bool(n):
        for i in range(parts[-1].shape[0]):
            out[:, columns(order[n + i], dim)] = parts[-1][i, 0]


def last_kernel(n, dim, width, order, below, above, *refs):
    parts, outs = refs[:-2], refs[-2:]
    tokens = outs[0].shape[0]

    def put(j, head, ref, i, at):
        cols = columns(head, dim)
        out = outs[j]
        low = ref[i, at, :width].astype(F32) + below[j, :, cols].astype(F32)
        high = ref[i, at, tokens - width :].astype(F32) + above[j, :, cols].astype(F32)
        out[:width, cols] = low.astype(BF16)
        out[width : tokens - width, cols] = ref[i, at, width : tokens - width]
        out[tokens - width :, cols] = high.astype(BF16)

    for j in range(2):
        for slot in range(n):
            put(j, order[slot], parts[0], slot, j)
        if len(parts) > bool(n):
            for i in range(parts[-1].shape[0]):
                put(j, order[n + i], parts[-1], i, 1 + j)


def call(name, kernel, ins, outs, flops):
    shapes = [jax.ShapeDtypeStruct(s, d) for s, d in outs]
    moved = sum(x.size * x.dtype.itemsize for x in list(ins) + shapes)
    return pl.pallas_call(
        kernel,
        out_shape=shapes,
        in_specs=[SMEM if x.dtype == jnp.int32 else VMEM for x in ins],
        out_specs=[SMEM if x.dtype == jnp.int32 else VMEM for x in shapes],
        cost_estimate=pl.CostEstimate(flops=flops, bytes_accessed=moved, transcendentals=0),
        compiler_params=pltpu.CompilerParams(vmem_limit_bytes=VMEM_LIMIT),
        name=name,
    )(*ins)


def run(n, heads, dim, width, args):
    q, g, k, v, reach, offs = args
    tokens, packed = q.shape
    part = functools.partial
    rim = ((2, width, packed), BF16)
    whole = ((tokens, packed), BF16)
    tile = (tokens, dim)
    longer = (tokens + 2 * width, dim)
    flops = 2 * longer[0] * tokens * dim
    rest = heads - n
    order, near, far = call(
        "edge", part(edge_kernel, heads, width), [reach, k, v],
        [((heads,), jnp.int32), rim, rim], 0,
    )
    near, far = swapped(near, "row", 0), swapped(far, "row", 1)
    grads_own = rims = None
    if n:
        (own,) = call(
            "extend", part(extend_kernel, n, dim, width), [order, k, v, near, far],
            [((n, 2) + longer, BF16)], 0,
        )
        prev, following = shifted(own, "frame", 1), shifted(own, "frame", -1)
        (own_q,) = call(
            "pack", part(pack_kernel, n, dim), [order, q, g], [((n, 2) + tile, BF16)], 0
        )
        q_prev, q_next = shifted(own_q, "frame", 1), shifted(own_q, "frame", -1)
    if rest:
        grads_own, rims = call(
            "own", part(own_kernel, n, heads, dim, width), [order, offs, q, g, k, v, near, far],
            [((rest, 3) + tile, BF16), ((rest, 2, 2, width, dim), BF16)], flops * 5 * rest,
        )
    more = [grads_own] if rest else []
    if n:
        grid = ((n, 3, tokens // 2 + width, tokens), F32)
        stats, s, dp = call(
            "query", part(query_kernel, n, dim, width),
            [order, reach, offs, own_q, own, prev, following],
            [((n // 2, 8, tokens), F32), grid, grid], flops * 6 * n,
        )
        st_prev, st_next = shifted(stats, "frame", 1), shifted(stats, "frame", -1)
        acc, dq = call(
            "finish", part(finish_kernel, n, dim, width),
            [order, reach, offs, own_q, own, prev, following, stats, s, dp],
            [((n, 2) + longer, F32), ((n,) + tile, BF16)], flops * 5 * n,
        )
        grads, rim_low, rim_high = call(
            "key", part(key_kernel, n, dim, width),
            [order, reach, offs, own, q_prev, q_next, st_prev, st_next, acc]
            + ([rims] if rest else []),
            [((n, 2) + tile, BF16), rim, rim], flops * 8 * n,
        )
        query_parts, key_parts = [dq] + more, [grads] + more
    else:
        rim_low, rim_high = call("rims", part(rim_kernel, dim), [order, rims], [rim, rim], 0)
        query_parts = key_parts = more
    below, above = shifted(rim_high, "row", 1), shifted(rim_low, "row", -1)
    (dq,) = call("dq", part(query_out_kernel, n, dim), [order] + query_parts, [whole], 0)
    dk, dv = call(
        "last", part(last_kernel, n, dim, width), [order, below, above] + key_parts,
        [whole, whole], 0,
    )
    return dq, dk, dv


def on_device(query_tok, key_tok, value_tok, grad_out, head_reach, tile_offset):
    block = query_tok.shape
    rows_dev, width, packed = block[1:]
    heads = head_reach.shape[0]
    dim = packed // heads
    flat = [x.reshape(rows_dev * width, packed) for x in (query_tok, grad_out, key_tok, value_tok)]
    args = flat + [head_reach, tile_offset]
    sizes = list(range(0, heads + 1, STEP))
    count = jnp.sum(head_reach)
    grads = lax.switch(
        (count + STEP - 1) // STEP,
        [functools.partial(run, n, heads, dim, width) for n in sizes],
        args,
    )
    return tuple(x.reshape(block) for x in grads)


def solution(mesh):
    spec = P("frame", "row", None, None)
    return jax.shard_map(
        on_device,
        mesh=mesh,
        in_specs=(spec, spec, spec, spec, P(), P(None, "row")),
        out_specs=(spec, spec, spec),
        check_vma=False,
    )
```

time: 101 us -> 86.4 us (0.86)
  the two profiles are of different devices: /device:TPU:199 before, /device:TPU:223 now
where the time goes in v2:
time: 86.4 us; the launch traced here: 85.8 us
  starting transfers between devices  33.2 us (38%)
  Pallas kernels  25.5 us (30%)
  waiting for transfers between devices  20.9 us (24%)
  local copies, waits for them, and re-layouts  3.29 us (4%)
  between operations  1.3 us (2%)
  other arithmetic  1.29 us (1%)
    pallas_call x9, Pallas kernels, call(): pl.pallas_call(kernel, out_shape=shapes, in_specs=[SMEM if x.dtype == jnp...  25.5 us
    ppermute x8, starting transfers between devices, shifted(): return lax.ppermute(block, axis, route)  25.4 us
    ppermute x8, waiting for transfers between devices, shifted(): return lax.ppermute(block, axis, route)  18 us
    ppermute x2, starting transfers between devices, swapped(): return lax.ppermute(block, axis, pairs + [(b, a) for a, b in pairs])  7.82 us
    ppermute x2, waiting for transfers between devices, swapped(): return lax.ppermute(block, axis, pairs + [(b, a) for a, b in pairs])  2.97 us
    cond x22, local copies, waits for them, and re-layouts  2.53 us
  transfers between devices with their start and end apart: 10, of which 6 were waited for; matrix products, arithmetic and copies ran while one was open for 1% of the time, Pallas kernels for 16%

profile of v2, /device:TPU:223, one launch (start us, length us, event | category | flops | bytes accessed | tf_op | source)
XLA Modules:
  0.0 85.8 jit_solution(241300287030576576)
XLA Ops:
  0.6 1.3 %reduce_sum.9 = s32[]{:T(128)} reduce(s32[20]{0:T(128)} %param.16, s32[]{:T(128)} %constant.16.clone.1), dimensions={0}, to_apply=%region_0.0 | reduce | flops 19 | bytes 88 | tf_op jit(solution)/shard_map/reduce_sum | solution.py:449
  2.6 83.2 %conditional.1 = (bf16[128,2560]{1,0:T(8,128)(2,1)}, bf16[128,2560]{1,0:T(8,128)(2,1)}, bf16[1,8,16,2560]{3,2,1,0:T(8,128)(2,1)}) conditional(s32[]{:T(128)} %clamp.3, (s32[20]{0:T(128)}, bf16[128,2560]{1,0:T(8,128)(2,1)}, bf16[128,2560]{1,0:T(8,128)(2,1)}, s32[32,2]{0,1:T(2,128)}, bf16[128,2560]{1,0:T(8,128)(2,1)}, ...), branch_computations={%region_1.2_spmd, %region_2.3_spmd, %region_3.4_spmd, %region_4.5_... | conditional | flops 1992294400 | bytes 84381776 | solution.py:450
  2.6 0.0 copy-start.13
  2.6 0.0 copy-start.19
  2.6 2.4 %edge.9 = (s32[20]{0:T(128)S(1)}, bf16[2,16,2560]{2,1,0:T(8,128)(2,1)S(1)}, bf16[2,16,2560]{2,1,0:T(8,128)(2,1)S(1)}) custom-call(s32[20]{0:T(128)} %get-tuple-element.130.reach, bf16[128,2560]{1,0:T(8,128)(2,1)} %get-tuple-element.131.k, bf16[128,2560]{1,0:T(8,128)(2,1)} %get-tuple-element.132.v), custom_call_target="tpu_custom_call" | custom-call | bytes 1638560 | tf_op jit(solution)/shard_map/cond/branch_3_fun/edge/pallas_call | solution.py:366
  5.0 0.0 copy-start.8
  5.0 0.0 copy-start.24
  5.0 0.0 copy-start.29
  5.1 2.7 %collective-permute-start.24 = (bf16[2,16,2560]{2,1,0:T(8,128)(2,1)S(1)}, bf16[2,16,2560]{2,1,0:T(8,128)(2,1)S(1)}, u32[]{:S(2)}, u32[]{:S(2)}) collective-permute-start(bf16[2,16,2560]{2,1,0:T(8,128)(2,1)S(1)} %get-tuple-element.135), channel_id=1, source_target_pairs={{0,1},{2,3},{4,5},{6,7},{8,9},{10,11},{12,13},{14,15},{1,0},{3,2},... | collective-permute-start | bytes 491528 | tf_op jit(solution)/shard_map/cond/branch_3_fun/ppermute | solution.py:27
  7.8 5.1 %collective-permute-start.25 = (bf16[2,16,2560]{2,1,0:T(8,128)(2,1)S(1)}, bf16[2,16,2560]{2,1,0:T(8,128)(2,1)S(1)}, u32[]{:S(2)}, u32[]{:S(2)}) collective-permute-start(bf16[2,16,2560]{2,1,0:T(8,128)(2,1)S(1)} %get-tuple-element.136), channel_id=1, source_target_pairs={{1,2},{3,4},{5,6},{7,8},{9,10},{11,12},{13,14},{2,1},{4,3},{6,5},{... | collective-permute-start | bytes 491528 | tf_op jit(solution)/shard_map/cond/branch_3_fun/ppermute | solution.py:27
  12.9 0.0 collective-permute-done.24.near
  12.9 0.0 copy-start
  12.9 3.0 %collective-permute-done.25.far = bf16[2,16,2560]{2,1,0:T(8,128)(2,1)S(1)} collective-permute-done((bf16[2,16,2560]{2,1,0:T(8,128)(2,1)S(1)}, bf16[2,16,2560]{2,1,0:T(8,128)(2,1)S(1)}, u32[]{:S(2)}, u32[]{:S(2)}) %collective-permute-start.25) | collective-permute-done | bytes 163872 | tf_op jit(solution)/shard_map/cond/branch_3_fun/ppermute | solution.py:27
  15.9 0.0 copy-done.13
  15.9 0.0 copy-done.19
  15.9 0.7 extend.7.own
  16.6 4.4 %collective-permute-start.28 = (bf16[12,2,160,128]{3,2,1,0:T(8,128)(2,1)S(1)}, bf16[12,2,160,128]{3,2,1,0:T(8,128)(2,1)S(1)}, u32[]{:S(2)}, u32[]{:S(2)}) collective-permute-start(bf16[12,2,160,128]{3,2,1,0:T(8,128)(2,1)S(1)} %extend.7.own), channel_id=1, source_target_pairs={{0,16},{16,32},{32,48},{48,64},{64,80},{80,96},{96,112},{112,128},... | collective-permute-start | bytes 2949128 | tf_op jit(solution)/shard_map/cond/branch_3_fun/ppermute | solution.py:21
  21.0 1.9 %collective-permute-start.29 = (bf16[12,2,160,128]{3,2,1,0:T(8,128)(2,1)S(1)}, bf16[12,2,160,128]{3,2,1,0:T(8,128)(2,1)}, u32[]{:S(2)}, u32[]{:S(2)}) collective-permute-start(bf16[12,2,160,128]{3,2,1,0:T(8,128)(2,1)S(1)} %extend.7.own), channel_id=1, source_target_pairs={{16,0},{32,16},{48,32},{64,48},{80,64},{96,80},{112,96},{128,112},... | collective-permute-start | bytes 2949128 | tf_op jit(solution)/shard_map/cond/branch_3_fun/ppermute | solution.py:21
  23.0 0.0 copy-done.24
  23.0 0.0 copy-done.29
  23.0 0.7 pack.7.own_q
  23.7 0.0 copy-done.8
  23.7 0.0 copy-done
  23.7 0.0 copy-done.4
  23.7 4.6 %collective-permute-start.26 = (bf16[12,2,128,128]{3,2,1,0:T(8,128)(2,1)S(1)}, bf16[12,2,128,128]{3,2,1,0:T(8,128)(2,1)S(1)}, u32[]{:S(2)}, u32[]{:S(2)}) collective-permute-start(bf16[12,2,128,128]{3,2,1,0:T(8,128)(2,1)S(1)} %pack.7.own_q), channel_id=1, source_target_pairs={{0,16},{16,32},{32,48},{48,64},{64,80},{80,96},{96,112},{112,128},... | collective-permute-start | bytes 2359304 | tf_op jit(solution)/shard_map/cond/branch_3_fun/ppermute | solution.py:21
  28.3 1.9 %collective-permute-start.27 = (bf16[12,2,128,128]{3,2,1,0:T(8,128)(2,1)S(1)}, bf16[12,2,128,128]{3,2,1,0:T(8,128)(2,1)}, u32[]{:S(2)}, u32[]{:S(2)}) collective-permute-start(bf16[12,2,128,128]{3,2,1,0:T(8,128)(2,1)S(1)} %pack.7.own_q), channel_id=1, source_target_pairs={{16,0},{32,16},{48,32},{64,48},{80,64},{96,80},{112,96},{128,112},... | collective-permute-start | bytes 2359304 | tf_op jit(solution)/shard_map/cond/branch_3_fun/ppermute | solution.py:21
  30.2 0.8 copy.12.offs
  31.0 0.9 %copy-done.1 = bf16[2,16,2560]{2,1,0:T(8,128)(2,1)S(1)} copy-done((bf16[2,16,2560]{2,1,0:T(8,128)(2,1)S(1)}, bf16[2,16,2560]{2,1,0:T(8,128)(2,1)}, u32[]{:S(2)}) %copy-start.1) | copy-done | bytes 163864 | tf_op jit(solution)/shard_map/cond
  31.9 0.9 %copy-done.5 = bf16[2,16,2560]{2,1,0:T(8,128)(2,1)S(1)} copy-done((bf16[2,16,2560]{2,1,0:T(8,128)(2,1)S(1)}, bf16[2,16,2560]{2,1,0:T(8,128)(2,1)}, u32[]{:S(2)}) %copy-start.5) | copy-done | bytes 163864 | tf_op jit(solution)/shard_map/cond
  32.8 0.7 copy-done.9
  33.5 4.7 %own.8 = (bf16[8,3,128,128]{3,2,1,0:T(8,128)(2,1)S(1)}, bf16[8,2,2,16,128]{4,3,2,1,0:T(8,128)(2,1)S(1)}) custom-call(s32[20]{0:T(128)S(1)} %copy-done.9, s32[32,2]{1,0:T(8,128)S(1)} %copy.12.offs, bf16[128,2560]{1,0:T(8,128)(2,1)} %get-tuple-element.137.q, bf16[128,2560]{1,0:T(8,128)(2,1)} %get-tuple-element.138.g, bf16[128,2560]{1,0:T(8,128)(2,1)} %get-tuple-element.131.k, ...), custom_call_target="tpu_custom_call" | custom-call | flops 209715200 | bytes 3866960 | tf_op jit(solution)/shard_map/cond/branch_3_fun/own/pallas_call | solution.py:366
  38.1 4.5 %collective-permute-done.28.prev = bf16[12,2,160,128]{3,2,1,0:T(8,128)(2,1)S(1)} collective-permute-done((bf16[12,2,160,128]{3,2,1,0:T(8,128)(2,1)S(1)}, bf16[12,2,160,128]{3,2,1,0:T(8,128)(2,1)S(1)}, u32[]{:S(2)}, u32[]{:S(2)}) %collective-permute-start.28) | collective-permute-done | bytes 983072 | tf_op jit(solution)/shard_map/cond/branch_3_fun/ppermute | solution.py:21
  42.6 5.4 %collective-permute-done.29.following = bf16[12,2,160,128]{3,2,1,0:T(8,128)(2,1)} collective-permute-done((bf16[12,2,160,128]{3,2,1,0:T(8,128)(2,1)S(1)}, bf16[12,2,160,128]{3,2,1,0:T(8,128)(2,1)}, u32[]{:S(2)}, u32[]{:S(2)}) %collective-permute-start.29) | collective-permute-done | bytes 983072 | tf_op jit(solution)/shard_map/cond/branch_3_fun/ppermute | solution.py:21
  48.0 3.9 %query.7 = (f32[6,8,128]{2,1,0:T(8,128)S(1)}, f32[12,3,80,128]{3,2,1,0:T(8,128)S(1)}, f32[12,3,80,128]{3,2,1,0:T(8,128)S(1)}) custom-call(s32[20]{0:T(128)S(1)} %copy-done.9, s32[20]{0:T(128)S(1)} %copy-done.34, s32[32,2]{1,0:T(8,128)S(1)} %copy.12.offs, bf16[12,2,128,128]{3,2,1,0:T(8,128)(2,1)S(1)} %pack.7.own_q, bf16[12,2,160,128]{3,2,1,0:T(8,128)(2,1)S(1)} %extend.7.own, ...), custom_call_target="tpu_custom_call" | custom-call | flops 377487360 | bytes 6709664 | tf_op jit(solution)/shard_map/cond/branch_3_fun/query/pallas_call | solution.py:366
  51.9 1.9 %collective-permute-start.30 = (f32[6,8,128]{2,1,0:T(8,128)S(1)}, f32[6,8,128]{2,1,0:T(8,128)S(1)}, u32[]{:S(2)}, u32[]{:S(2)}) collective-permute-start(f32[6,8,128]{2,1,0:T(8,128)S(1)} %get-tuple-element.139.stats), channel_id=1, source_target_pairs={{0,16},{16,32},{32,48},{48,64},{64,80},{80,96},{96,112},{112,128},... | collective-permute-start | bytes 73736 | tf_op jit(solution)/shard_map/cond/branch_3_fun/ppermute | solution.py:21
  53.8 3.4 %collective-permute-start.31 = (f32[6,8,128]{2,1,0:T(8,128)S(1)}, f32[6,8,128]{2,1,0:T(8,128)S(1)}, u32[]{:S(2)}, u32[]{:S(2)}) collective-permute-start(f32[6,8,128]{2,1,0:T(8,128)S(1)} %get-tuple-element.139.stats), channel_id=1, source_target_pairs={{16,0},{32,16},{48,32},{64,48},{80,64},{96,80},{112,96},{128,112},... | collective-permute-start | bytes 73736 | tf_op jit(solution)/shard_map/cond/branch_3_fun/ppermute | solution.py:21
  57.2 3.4 %finish.7 = (f32[12,2,160,128]{3,2,1,0:T(8,128)S(1)}, bf16[12,128,128]{2,1,0:T(8,128)(2,1)S(1)}) custom-call(s32[20]{0:T(128)S(1)} %copy-done.9, s32[20]{0:T(128)S(1)} %copy-done.34, s32[32,2]{1,0:T(8,128)S(1)} %copy.12.offs, bf16[12,2,128,128]{3,2,1,0:T(8,128)(2,1)S(1)} %pack.7.own_q, bf16[12,2,160,128]{3,2,1,0:T(8,128)(2,1)S(1)} %extend.7.own, ...), custom_call_target="tpu_custom_call" | custom-call | flops 314572800 | bytes 9068960 | tf_op jit(solution)/shard_map/cond/branch_3_fun/finish/pallas_call | solution.py:366
  60.6 0.0 collective-permute-done.26.q_prev
  60.6 3.5 %collective-permute-done.27.q_next = bf16[12,2,128,128]{3,2,1,0:T(8,128)(2,1)} collective-permute-done((bf16[12,2,128,128]{3,2,1,0:T(8,128)(2,1)S(1)}, bf16[12,2,128,128]{3,2,1,0:T(8,128)(2,1)}, u32[]{:S(2)}, u32[]{:S(2)}) %collective-permute-start.27) | collective-permute-done | bytes 786464 | tf_op jit(solution)/shard_map/cond/branch_3_fun/ppermute | solution.py:21
  64.1 0.0 collective-permute-done.30.st_prev
  64.1 0.2 collective-permute-done.31.st_next
  64.3 6.5 %key.7 = (bf16[12,2,128,128]{3,2,1,0:T(8,128)(2,1)S(1)}, bf16[2,16,2560]{2,1,0:T(8,128)(2,1)S(1)}, bf16[2,16,2560]{2,1,0:T(8,128)(2,1)S(1)}) custom-call(s32[20]{0:T(128)S(1)} %copy-done.9, s32[20]{0:T(128)S(1)} %copy-done.34, s32[32,2]{1,0:T(8,128)S(1)} %copy.12.offs, bf16[12,2,160,128]{3,2,1,0:T(8,128)(2,1)S(1)} %extend.7.own, ...), custom_call_target="tpu_custom_call" | custom-call | flops 503316480 | bytes 5816736 | tf_op jit(solution)/shard_map/cond/branch_3_fun/key/pallas_call | solution.py:366
  70.8 5.3 %collective-permute-start.32 = (bf16[2,16,2560]{2,1,0:T(8,128)(2,1)S(1)}, bf16[2,16,2560]{2,1,0:T(8,128)(2,1)S(1)}, u32[]{:S(2)}, u32[]{:S(2)}) collective-permute-start(bf16[2,16,2560]{2,1,0:T(8,128)(2,1)S(1)} %get-tuple-element.144), channel_id=1, source_target_pairs={{0,1},{1,2},{2,3},{3,4},{4,5},{5,6},{6,7},{7,8},{8,9},{9,10},{10,1... | collective-permute-start | bytes 491528 | tf_op jit(solution)/shard_map/cond/branch_3_fun/ppermute | solution.py:21
  76.1 1.9 %collective-permute-start.33 = (bf16[2,16,2560]{2,1,0:T(8,128)(2,1)S(1)}, bf16[2,16,2560]{2,1,0:T(8,128)(2,1)S(1)}, u32[]{:S(2)}, u32[]{:S(2)}) collective-permute-start(bf16[2,16,2560]{2,1,0:T(8,128)(2,1)S(1)} %get-tuple-element.145), channel_id=1, source_target_pairs={{1,0},{2,1},{3,2},{4,3},{5,4},{6,5},{7,6},{8,7},{9,8},{10,9},{11,1... | collective-permute-start | bytes 491528 | tf_op jit(solution)/shard_map/cond/branch_3_fun/ppermute | solution.py:21
  78.0 1.5 %dq.9 = bf16[128,2560]{1,0:T(8,128)(2,1)} custom-call(s32[20]{0:T(128)S(1)} %copy-done.9, bf16[12,128,128]{2,1,0:T(8,128)(2,1)S(1)} %get-tuple-element.150.refs_0_, bf16[8,3,128,128]{3,2,1,0:T(8,128)(2,1)S(1)} %get-tuple-element.147.refs_1_), custom_call_target="tpu_custom_call" | custom-call | bytes 1835088 | tf_op jit(solution)/shard_map/cond/branch_3_fun/dq/pallas_call | solution.py:366
  79.6 0.0 collective-permute-done.32.below
  79.6 4.4 %collective-permute-done.33.above = bf16[2,16,2560]{2,1,0:T(8,128)(2,1)S(1)} collective-permute-done((bf16[2,16,2560]{2,1,0:T(8,128)(2,1)S(1)}, bf16[2,16,2560]{2,1,0:T(8,128)(2,1)S(1)}, u32[]{:S(2)}, u32[]{:S(2)}) %collective-permute-start.33) | collective-permute-done | bytes 163872 | tf_op jit(solution)/shard_map/cond/branch_3_fun/ppermute | solution.py:21
  84.0 1.8 %last.9 = (bf16[128,2560]{1,0:T(8,128)(2,1)}, bf16[128,2560]{1,0:T(8,128)(2,1)}) custom-call(s32[20]{0:T(128)S(1)} %copy-done.9, bf16[2,16,2560]{2,1,0:T(8,128)(2,1)S(1)} %collective-permute-done.32.below, bf16[2,16,2560]{2,1,0:T(8,128)(2,1)S(1)} %collective-permute-done.33.above, bf16[12,2,128,128]{3,2,1,0:T(8,128)(2,1)S(1)} %get-tuple-element.146.refs_0_, ...), custom_call_target="tpu_custom_call" | custom-call | bytes 3211344 | tf_op jit(solution)/shard_map/cond/branch_3_fun/last/pallas_call | solution.py:366
  (6 shorter events, 0.0 us)
Async XLA Ops:
  2.6 13.3 %copy-start.13 = (bf16[128,2560]{1,0:T(8,128)(2,1)S(1)}, bf16[128,2560]{1,0:T(8,128)(2,1)}, u32[]{:S(2)}) copy-start(bf16[128,2560]{1,0:T(8,128)(2,1)} %get-tuple-element.131.k) | copy-start | bytes 1966084 | tf_op jit(solution)/shard_map/cond
  2.6 13.3 %copy-start.19 = (bf16[128,2560]{1,0:T(8,128)(2,1)S(1)}, bf16[128,2560]{1,0:T(8,128)(2,1)}, u32[]{:S(2)}) copy-start(bf16[128,2560]{1,0:T(8,128)(2,1)} %get-tuple-element.132.v) | copy-start | bytes 1966084 | tf_op jit(solution)/shard_map/cond
  5.0 18.7 %copy-start.8 = (s32[20]{0:T(128)}, s32[20]{0:T(128)S(1)}, u32[]{:S(2)}) copy-start(s32[20]{0:T(128)S(1)} %get-tuple-element.133.order) | copy-start | bytes 244 | tf_op jit(solution)/shard_map/cond
  5.0 17.9 %copy-start.24 = (bf16[128,2560]{1,0:T(8,128)(2,1)S(1)}, bf16[128,2560]{1,0:T(8,128)(2,1)}, u32[]{:S(2)}) copy-start(bf16[128,2560]{1,0:T(8,128)(2,1)} %get-tuple-element.137.q) | copy-start | bytes 1966084 | tf_op jit(solution)/shard_map/cond
  5.0 17.9 %copy-start.29 = (bf16[128,2560]{1,0:T(8,128)(2,1)S(1)}, bf16[128,2560]{1,0:T(8,128)(2,1)}, u32[]{:S(2)}) copy-start(bf16[128,2560]{1,0:T(8,128)(2,1)} %get-tuple-element.138.g) | copy-start | bytes 1966084 | tf_op jit(solution)/shard_map/cond
  5.1 7.8 %collective-permute-start.24 = (bf16[2,16,2560]{2,1,0:T(8,128)(2,1)S(1)}, bf16[2,16,2560]{2,1,0:T(8,128)(2,1)S(1)}, u32[]{:S(2)}, u32[]{:S(2)}) collective-permute-start(bf16[2,16,2560]{2,1,0:T(8,128)(2,1)S(1)} %get-tuple-element.135), channel_id=1, source_target_pairs={{0,1},{2,3},{4,5},{6,7},{8,9},{10,11},{12,13},{14,15},{1,0},{3,2},... | collective-permute-start | bytes 491528 | tf_op jit(solution)/shard_map/cond/branch_3_fun/ppermute | solution.py:27
  7.8 8.1 %collective-permute-start.25 = (bf16[2,16,2560]{2,1,0:T(8,128)(2,1)S(1)}, bf16[2,16,2560]{2,1,0:T(8,128)(2,1)S(1)}, u32[]{:S(2)}, u32[]{:S(2)}) collective-permute-start(bf16[2,16,2560]{2,1,0:T(8,128)(2,1)S(1)} %get-tuple-element.136), channel_id=1, source_target_pairs={{1,2},{3,4},{5,6},{7,8},{9,10},{11,12},{13,14},{2,1},{4,3},{6,5},{... | collective-permute-start | bytes 491528 | tf_op jit(solution)/shard_map/cond/branch_3_fun/ppermute | solution.py:27
  12.9 10.8 %copy-start = (bf16[2,16,2560]{2,1,0:T(8,128)(2,1)}, bf16[2,16,2560]{2,1,0:T(8,128)(2,1)S(1)}, u32[]{:S(2)}) copy-start(bf16[2,16,2560]{2,1,0:T(8,128)(2,1)S(1)} %collective-permute-done.24.near) | copy-start | bytes 491524 | tf_op jit(solution)/shard_map/cond
  15.9 7.8 %copy-start.4 = (bf16[2,16,2560]{2,1,0:T(8,128)(2,1)}, bf16[2,16,2560]{2,1,0:T(8,128)(2,1)S(1)}, u32[]{:S(2)}) copy-start(bf16[2,16,2560]{2,1,0:T(8,128)(2,1)S(1)} %collective-permute-done.25.far) | copy-start | bytes 491524 | tf_op jit(solution)/shard_map/cond
  16.6 26.0 %collective-permute-start.28 = (bf16[12,2,160,128]{3,2,1,0:T(8,128)(2,1)S(1)}, bf16[12,2,160,128]{3,2,1,0:T(8,128)(2,1)S(1)}, u32[]{:S(2)}, u32[]{:S(2)}) collective-permute-start(bf16[12,2,160,128]{3,2,1,0:T(8,128)(2,1)S(1)} %extend.7.own), channel_id=1, source_target_pairs={{0,16},{16,32},{32,48},{48,64},{64,80},{80,96},{96,112},{112,128},... | collective-permute-start | bytes 2949128 | tf_op jit(solution)/shard_map/cond/branch_3_fun/ppermute | solution.py:21
  21.0 27.0 %collective-permute-start.29 = (bf16[12,2,160,128]{3,2,1,0:T(8,128)(2,1)S(1)}, bf16[12,2,160,128]{3,2,1,0:T(8,128)(2,1)}, u32[]{:S(2)}, u32[]{:S(2)}) collective-permute-start(bf16[12,2,160,128]{3,2,1,0:T(8,128)(2,1)S(1)} %extend.7.own), channel_id=1, source_target_pairs={{16,0},{32,16},{48,32},{64,48},{80,64},{96,80},{112,96},{128,112},... | collective-permute-start | bytes 2949128 | tf_op jit(solution)/shard_map/cond/branch_3_fun/ppermute | solution.py:21
  23.7 36.9 %collective-permute-start.26 = (bf16[12,2,128,128]{3,2,1,0:T(8,128)(2,1)S(1)}, bf16[12,2,128,128]{3,2,1,0:T(8,128)(2,1)S(1)}, u32[]{:S(2)}, u32[]{:S(2)}) collective-permute-start(bf16[12,2,128,128]{3,2,1,0:T(8,128)(2,1)S(1)} %pack.7.own_q), channel_id=1, source_target_pairs={{0,16},{16,32},{32,48},{48,64},{64,80},{80,96},{96,112},{112,128},... | collective-permute-start | bytes 2359304 | tf_op jit(solution)/shard_map/cond/branch_3_fun/ppermute | solution.py:21
  28.3 35.8 %collective-permute-start.27 = (bf16[12,2,128,128]{3,2,1,0:T(8,128)(2,1)S(1)}, bf16[12,2,128,128]{3,2,1,0:T(8,128)(2,1)}, u32[]{:S(2)}, u32[]{:S(2)}) collective-permute-start(bf16[12,2,128,128]{3,2,1,0:T(8,128)(2,1)S(1)} %pack.7.own_q), channel_id=1, source_target_pairs={{16,0},{32,16},{48,32},{64,48},{80,64},{96,80},{112,96},{128,112},... | collective-permute-start | bytes 2359304 | tf_op jit(solution)/shard_map/cond/branch_3_fun/ppermute | solution.py:21
  31.0 0.9 %copy-start.1 = (bf16[2,16,2560]{2,1,0:T(8,128)(2,1)S(1)}, bf16[2,16,2560]{2,1,0:T(8,128)(2,1)}, u32[]{:S(2)}) copy-start(bf16[2,16,2560]{2,1,0:T(8,128)(2,1)} %copy-done) | copy-start | bytes 491524 | tf_op jit(solution)/shard_map/cond
  31.9 0.9 %copy-start.5 = (bf16[2,16,2560]{2,1,0:T(8,128)(2,1)S(1)}, bf16[2,16,2560]{2,1,0:T(8,128)(2,1)}, u32[]{:S(2)}) copy-start(bf16[2,16,2560]{2,1,0:T(8,128)(2,1)} %copy-done.4) | copy-start | bytes 491524 | tf_op jit(solution)/shard_map/cond
  32.8 0.7 copy-start.9
  33.5 14.5 %copy-start.34 = (s32[20]{0:T(128)S(1)}, s32[20]{0:T(128)}, u32[]{:S(2)}) copy-start(s32[20]{0:T(128)} %get-tuple-element.130.reach) | copy-start | bytes 244 | tf_op jit(solution)/shard_map/cond
  51.9 12.2 %collective-permute-start.30 = (f32[6,8,128]{2,1,0:T(8,128)S(1)}, f32[6,8,128]{2,1,0:T(8,128)S(1)}, u32[]{:S(2)}, u32[]{:S(2)}) collective-permute-start(f32[6,8,128]{2,1,0:T(8,128)S(1)} %get-tuple-element.139.stats), channel_id=1, source_target_pairs={{0,16},{16,32},{32,48},{48,64},{64,80},{80,96},{96,112},{112,128},... | collective-permute-start | bytes 73736 | tf_op jit(solution)/shard_map/cond/branch_3_fun/ppermute | solution.py:21
  53.8 10.5 %collective-permute-start.31 = (f32[6,8,128]{2,1,0:T(8,128)S(1)}, f32[6,8,128]{2,1,0:T(8,128)S(1)}, u32[]{:S(2)}, u32[]{:S(2)}) collective-permute-start(f32[6,8,128]{2,1,0:T(8,128)S(1)} %get-tuple-element.139.stats), channel_id=1, source_target_pairs={{16,0},{32,16},{48,32},{64,48},{80,64},{96,80},{112,96},{128,112},... | collective-permute-start | bytes 73736 | tf_op jit(solution)/shard_map/cond/branch_3_fun/ppermute | solution.py:21
  70.8 8.8 %collective-permute-start.32 = (bf16[2,16,2560]{2,1,0:T(8,128)(2,1)S(1)}, bf16[2,16,2560]{2,1,0:T(8,128)(2,1)S(1)}, u32[]{:S(2)}, u32[]{:S(2)}) collective-permute-start(bf16[2,16,2560]{2,1,0:T(8,128)(2,1)S(1)} %get-tuple-element.144), channel_id=1, source_target_pairs={{0,1},{1,2},{2,3},{3,4},{4,5},{5,6},{6,7},{7,8},{8,9},{9,10},{10,1... | collective-permute-start | bytes 491528 | tf_op jit(solution)/shard_map/cond/branch_3_fun/ppermute | solution.py:21
  76.1 7.8 %collective-permute-start.33 = (bf16[2,16,2560]{2,1,0:T(8,128)(2,1)S(1)}, bf16[2,16,2560]{2,1,0:T(8,128)(2,1)S(1)}, u32[]{:S(2)}, u32[]{:S(2)}) collective-permute-start(bf16[2,16,2560]{2,1,0:T(8,128)(2,1)S(1)} %get-tuple-element.145), channel_id=1, source_target_pairs={{1,0},{2,1},{3,2},{4,3},{5,4},{6,5},{7,6},{8,7},{9,8},{10,9},{11,1... | collective-permute-start | bytes 491528 | tf_op jit(solution)/shard_map/cond/branch_3_fun/ppermute | solution.py:21

commit v3 on v2

--- a/solution.py
+++ b/solution.py
@@ -8,11 +8,16 @@
 from jax.experimental.pallas import tpu as pltpu
 from jax.sharding import PartitionSpec as P
 
-STEP = 4
-VMEM_LIMIT = 24 << 20
+
+SIZES = (4, 6, 8, 10, 12, 14, 16, 20)
+VMEM_LIMIT = 16 << 20
 F32, BF16 = jnp.float32, jnp.bfloat16
 SMEM = pl.BlockSpec(memory_space=pltpu.SMEM)
 VMEM = pl.BlockSpec(memory_space=pltpu.VMEM)
+
+
+def both(block):
+    return shifted(block, "frame", 1), shifted(block, "frame", -1)
 
 
 def shifted(block, axis, distance):
@@ -78,9 +83,8 @@
         edge1 = jnp.where(offs[1], main[half - width : half], high)
         return jnp.concatenate([main, edge0, edge1], axis=0)
 
-    def keys_of(self, extended, offs):
-        width, end = self.width, self.width + self.tokens
-        return self.keys(extended[width:end], extended[:width], extended[end:], offs)
+    def keys_of(self, main, rims, slot, j, offs):
+        return self.keys(main[slot, j], rims[slot, j, 0], rims[slot, j, 1], offs)
 
     def by_tile(self, product):
         half, width, tokens = self.half, self.width, self.tokens
@@ -161,13 +165,17 @@
     return top, inverse, weighted * inverse
 
 
-def edge_kernel(heads, width, reach, k, v, order, near, far):
+def each(count, body):
+    def step(i, carry):
+        body(i)
+        return carry
+
+    lax.fori_loop(0, count, step, 0)
+
+
+def first_kernel(n, heads, dim, width, reach, k, v, order, near, far, *rest):
     tokens = k.shape[0]
     even = lax.rem(lax.axis_index("row"), 2) == 0
-    for j, ref in enumerate((k, v)):
-        first, last = ref[:width], ref[tokens - width :]
-        near[j] = jnp.where(even, last, first)
-        far[j] = jnp.where(even, first, last)
     count = lax.fori_loop(0, heads, lambda h, c: c + reach[h], 0)
 
     def place(h, carry):
@@ -178,24 +186,41 @@
 
     lax.fori_loop(0, heads, place, (0, count))
 
-
-def pack_kernel(n, dim, order, q, g, send):
-    for slot in range(n):
+    def pack(slot):
+        cols = columns(order[slot], dim)
+        for j, ref in enumerate((k, v)):
+            rest[0][slot, j] = ref[:, cols]
+
+    if n:
+        each(n, pack)
+    for j, ref in enumerate((k, v)):
+        first, last = ref[:width], ref[tokens - width :]
+        near[j] = jnp.where(even, last, first)
+        far[j] = jnp.where(even, first, last)
+
+
+def pack_kernel(n, dim, order, q, g, rims, send):
+    del rims
+
+    def pack(slot):
         cols = columns(order[slot], dim)
         send[slot, 0] = q[:, cols]
         send[slot, 1] = g[:, cols]
 
-
-def extend_kernel(n, dim, width, order, k, v, near, far, send):
-    tokens = k.shape[0]
-    geo = Geometry(tokens, width, dim)
-    for slot in range(n):
+    each(n, pack)
+
+
+def rims_kernel(n, dim, width, order, near, far, send):
+    geo = Geometry(8 * width, width, dim)
+
+    def pack(slot):
         cols = columns(order[slot], dim)
-        for j, ref in enumerate((k, v)):
+        for j in range(2):
             low, high = geo.rims(near[j, :, cols], far[j, :, cols])
-            send[slot, j, :width] = low
-            send[slot, j, width : width + tokens] = ref[:, cols]
-            send[slot, j, width + tokens :] = high
+            send[slot, j, 0] = low
+            send[slot, j, 1] = high
+
+    each(n, pack)
 
 
 def own_kernel(n, heads, dim, width, order, offs, q, g, k, v, near, far, grads, rims):
@@ -227,7 +252,10 @@
     lax.fori_loop(0, (heads - n) // 2, finish, 0)
 
 
-def query_kernel(n, dim, width, order, reach, offs, own_q, own, prev, following, stats, s_out, dp_out):
+def query_kernel(
+    n, dim, width, order, reach, offs, own_q, own, prev, following,
+    own_r, prev_r, next_r, stats, s_out, dp_out,
+):
     geo = Geometry(own_q.shape[2], width, dim)
     where = geo.offsets(offs, geo.frame)
     has_prev, has_next = geo.has(geo.frame - 1), geo.has(geo.frame + 1)
@@ -237,9 +265,11 @@
             slot = 2 * pair + side
             on = reach[order[slot]] == 1
             parts = []
-            for i, block in enumerate((own, prev, following)):
-                keys = geo.keys_of(block[slot, 0], where)
-                values = geo.keys_of(block[slot, 1], where)
+            for i, (block, rims) in enumerate(
+                ((own, own_r), (prev, prev_r), (following, next_r))
+            ):
+                keys = geo.keys_of(block, rims, slot, 0, where)
+                values = geo.keys_of(block, rims, slot, 1, where)
                 s, dp = geo.scores(keys, values, own_q[slot, 0], own_q[slot, 1], where)
                 s_out[slot, i] = s
                 dp_out[slot, i] = dp
@@ -251,7 +281,8 @@
 
 
 def finish_kernel(
-    n, dim, width, order, reach, offs, own_q, own, prev, following, stats, s_in, dp_in, acc, dq
+    n, dim, width, order, reach, offs, own_q, own, prev, following,
+    own_r, prev_r, next_r, stats, s_in, dp_in, acc, dq,
 ):
     geo = Geometry(own_q.shape[2], width, dim)
     where = geo.offsets(offs, geo.frame)
@@ -263,10 +294,14 @@
             on = reach[order[slot]] == 1
             top, inverse, delta = get_stats(stats, pair, side)
             total = None
-            for i, (block, ok) in enumerate(
-                ((own, None), (prev, on & has_prev), (following, on & has_next))
+            for i, (block, rims, ok) in enumerate(
+                (
+                    (own, own_r, None),
+                    (prev, prev_r, on & has_prev),
+                    (following, next_r, on & has_next),
+                )
             ):
-                keys = geo.keys_of(block[slot, 0], where)
+                keys = geo.keys_of(block, rims, slot, 0, where)
                 part = inverse if ok is None else jnp.where(ok, inverse, jnp.float32(0.0))
                 s = s_in[slot, i] if ok is None else jnp.minimum(s_in[slot, i], top)
                 weights, dscores = geo.weigh(s, dp_in[slot, i], top, part, delta)
@@ -282,7 +317,7 @@
 
 
 def key_kernel(
-    n, dim, width, order, reach, offs, own, q_prev, q_next, st_prev, st_next, acc, *refs
+    n, dim, width, order, reach, offs, own, own_r, q_prev, q_next, st_prev, st_next, acc, *refs
 ):
     tokens = q_prev.shape[2]
     geo = Geometry(tokens, width, dim)
@@ -296,8 +331,8 @@
             total = [acc[slot, 0], acc[slot, 1]]
             for step, queries, stats in ((-1, q_prev, st_prev), (1, q_next, st_next)):
                 where = geo.offsets(offs, geo.frame + step)
-                keys = geo.keys_of(own[slot, 0], where)
-                values = geo.keys_of(own[slot, 1], where)
+                keys = geo.keys_of(own, own_r, slot, 0, where)
+                values = geo.keys_of(own, own_r, slot, 1, where)
                 query, grad = queries[slot, 0], queries[slot, 1]
                 s, dp = geo.scores(keys, values, query, grad, where)
                 top, inverse, delta = get_stats(stats, pair, side)
@@ -319,12 +354,14 @@
 
 
 def spread_rims(n, order, rims, rim_low, rim_high, dim):
-    for i in range(rims.shape[0]):
+    def put(i):
         cols = columns(order[n + i], dim)
         for j in range(2):
             rim_low[j, :, cols] = rims[i, 0, j]
             rim_high[j, :, cols] = rims[i, 1, j]
 
+    each(rims.shape[0], put)
+
 
 def rim_kernel(dim, order, rims, rim_low, rim_high):
     spread_rims(0, order, rims, rim_low, rim_high, dim)
@@ -332,11 +369,17 @@
 
 def query_out_kernel(n, dim, order, *refs):
     parts, out = refs[:-1], refs[-1]
-    for slot in range(n):
+
+    def active(slot):
         out[:, columns(order[slot], dim)] = parts[0][slot]
+
+    def passive(i):
+        out[:, columns(order[n + i], dim)] = parts[-1][i, 0]
+
+    if n:
+        each(n, active)
     if len(parts) > bool(n):
-        for i in range(parts[-1].shape[0]):
-            out[:, columns(order[n + i], dim)] = parts[-1][i, 0]
+        each(parts[-1].shape[0], passive)
 
 
 def last_kernel(n, dim, width, order, below, above, *refs):
@@ -352,15 +395,21 @@
         out[width : tokens - width, cols] = ref[i, at, width : tokens - width]
         out[tokens - width :, cols] = high.astype(BF16)
 
-    for j in range(2):
-        for slot in range(n):
+    def active(slot):
+        for j in range(2):
             put(j, order[slot], parts[0], slot, j)
-        if len(parts) > bool(n):
-            for i in range(parts[-1].shape[0]):
-                put(j, order[n + i], parts[-1], i, 1 + j)
-
-
-def call(name, kernel, ins, outs, flops):
+
+    def passive(i):
+        for j in range(2):
+            put(j, order[n + i], parts[-1], i, 1 + j)
+
+    if n:
+        each(n, active)
+    if len(parts) > bool(n):
+        each(parts[-1].shape[0], passive)
+
+
+def call(kernel, ins, outs, flops):
     shapes = [jax.ShapeDtypeStruct(s, d) for s, d in outs]
     moved = sum(x.size * x.dtype.itemsize for x in list(ins) + shapes)
     return pl.pallas_call(
@@ -370,11 +419,14 @@
         out_specs=[SMEM if x.dtype == jnp.int32 else VMEM for x in shapes],
         cost_estimate=pl.CostEstimate(flops=flops, bytes_accessed=moved, transcendentals=0),
         compiler_params=pltpu.CompilerParams(vmem_limit_bytes=VMEM_LIMIT),
-        name=name,
     )(*ins)
 
 
-def run(n, heads, dim, width, args):
+def run(n, *rest):
+    return steps(n, *rest)
+
+
+def steps(n, heads, dim, width, args):
     q, g, k, v, reach, offs = args
     tokens, packed = q.shape
     part = functools.partial
@@ -384,55 +436,57 @@
     longer = (tokens + 2 * width, dim)
     flops = 2 * longer[0] * tokens * dim
     rest = heads - n
-    order, near, far = call(
-        "edge", part(edge_kernel, heads, width), [reach, k, v],
-        [((heads,), jnp.int32), rim, rim], 0,
+    packs = ((n, 2) + tile, BF16)
+    order, near, far, *own = call(
+        part(first_kernel, n, heads, dim, width), [reach, k, v],
+        [((heads,), jnp.int32), rim, rim] + ([packs] if n else []), 0,
     )
-    near, far = swapped(near, "row", 0), swapped(far, "row", 1)
     grads_own = rims = None
     if n:
-        (own,) = call(
-            "extend", part(extend_kernel, n, dim, width), [order, k, v, near, far],
-            [((n, 2) + longer, BF16)], 0,
-        )
-        prev, following = shifted(own, "frame", 1), shifted(own, "frame", -1)
-        (own_q,) = call(
-            "pack", part(pack_kernel, n, dim), [order, q, g], [((n, 2) + tile, BF16)], 0
-        )
-        q_prev, q_next = shifted(own_q, "frame", 1), shifted(own_q, "frame", -1)
+        own = own[0]
+        prev, following = both(own)
+    near, far = swapped(near, "row", 0), swapped(far, "row", 1)
+    if n:
+        (own_r,) = call(
+            part(rims_kernel, n, dim, width), [order, near, far],
+            [((n, 2, 2, width, dim), BF16)], 0,
+        )
+        prev_r, next_r = both(own_r)
+        (own_q,) = call(part(pack_kernel, n, dim), [order, q, g, own_r], [packs], 0)
+        q_prev, q_next = both(own_q)
     if rest:
         grads_own, rims = call(
-            "own", part(own_kernel, n, heads, dim, width), [order, offs, q, g, k, v, near, far],
+            part(own_kernel, n, heads, dim, width), [order, offs, q, g, k, v, near, far],
             [((rest, 3) + tile, BF16), ((rest, 2, 2, width, dim), BF16)], flops * 5 * rest,
         )
     more = [grads_own] if rest else []
     if n:
         grid = ((n, 3, tokens // 2 + width, tokens), F32)
         stats, s, dp = call(
-            "query", part(query_kernel, n, dim, width),
-            [order, reach, offs, own_q, own, prev, following],
+            part(query_kernel, n, dim, width),
+            [order, reach, offs, own_q, own, prev, following, own_r, prev_r, next_r],
             [((n // 2, 8, tokens), F32), grid, grid], flops * 6 * n,
         )
         st_prev, st_next = shifted(stats, "frame", 1), shifted(stats, "frame", -1)
         acc, dq = call(
-            "finish", part(finish_kernel, n, dim, width),
-            [order, reach, offs, own_q, own, prev, following, stats, s, dp],
+            part(finish_kernel, n, dim, width),
+            [order, reach, offs, own_q, own, prev, following, own_r, prev_r, next_r, stats, s, dp],
             [((n, 2) + longer, F32), ((n,) + tile, BF16)], flops * 5 * n,
         )
         grads, rim_low, rim_high = call(
-            "key", part(key_kernel, n, dim, width),
-            [order, reach, offs, own, q_prev, q_next, st_prev, st_next, acc]
+            part(key_kernel, n, dim, width),
+            [order, reach, offs, own, own_r, q_prev, q_next, st_prev, st_next, acc]
             + ([rims] if rest else []),
             [((n, 2) + tile, BF16), rim, rim], flops * 8 * n,
         )
         query_parts, key_parts = [dq] + more, [grads] + more
     else:
-        rim_low, rim_high = call("rims", part(rim_kernel, dim), [order, rims], [rim, rim], 0)
+        rim_low, rim_high = call(part(rim_kernel, dim), [order, rims], [rim, rim], 0)
         query_parts = key_parts = more
     below, above = shifted(rim_high, "row", 1), shifted(rim_low, "row", -1)
-    (dq,) = call("dq", part(query_out_kernel, n, dim), [order] + query_parts, [whole], 0)
+    (dq,) = call(part(query_out_kernel, n, dim), [order] + query_parts, [whole], 0)
     dk, dv = call(
-        "last", part(last_kernel, n, dim, width), [order, below, above] + key_parts,
+        part(last_kernel, n, dim, width), [order, below, above] + key_parts,
         [whole, whole], 0,
     )
     return dq, dk, dv
@@ -445,11 +499,10 @@
     dim = packed // heads
     flat = [x.reshape(rows_dev * width, packed) for x in (query_tok, grad_out, key_tok, value_tok)]
     args = flat + [head_reach, tile_offset]
-    sizes = list(range(0, heads + 1, STEP))
     count = jnp.sum(head_reach)
     grads = lax.switch(
-        (count + STEP - 1) // STEP,
-        [functools.partial(run, n, heads, dim, width) for n in sizes],
+        sum((count > n).astype(jnp.int32) for n in SIZES[:-1]),
+        [functools.partial(run, n, heads, dim, width) for n in SIZES],
         args,
     )
     return tuple(x.reshape(block) for x in grads)

time: 86.4 us -> 96.1 us (1.11)
  the two profiles are of different devices: /device:TPU:223 before, /device:TPU:199 now
where the time goes in v3:
time: 96.1 us; the launch traced here: 95.6 us
  starting transfers between devices  43 us (45%)
  Pallas kernels  24.2 us (25%)
  waiting for transfers between devices  21.5 us (22%)
  between operations  5.17 us (5%)
  other arithmetic  1.29 us (1%)
    ppermute x10, starting transfers between devices, shifted(): return lax.ppermute(block, axis, route)  35.3 us
    pallas_call x9, Pallas kernels, call(): pl.pallas_call(kernel, out_shape=shapes, in_specs=[SMEM if x.dtype == jnp...  24.2 us
    ppermute x10, waiting for transfers between devices, shifted(): return lax.ppermute(block, axis, route)  21.5 us
    ppermute x2, starting transfers between devices, swapped(): return lax.ppermute(block, axis, pairs + [(b, a) for a, b in pairs])  7.69 us
  transfers between devices with their start and end apart: 12, of which 2 were waited for; matrix products, arithmetic and copies ran while one was open for 0% of the time, Pallas kernels for 15%

profile of v3, /device:TPU:199, one launch (start us, length us, event | category | flops | bytes accessed | tf_op | source)
XLA Modules:
  0.0 95.6 jit_solution(15655459152151266868)
XLA Ops:
  0.6 1.3 %reduce_sum.9 = s32[]{:T(128)} reduce(s32[20]{0:T(128)} %param.18, s32[]{:T(128)} %constant.0.clone.1), dimensions={0}, to_apply=%region_0.0 | reduce | flops 19 | bytes 88 | tf_op jit(solution)/shard_map/reduce_sum | solution.py:502
  6.5 89.1 %conditional.1 = (bf16[128,2560]{1,0:T(8,128)(2,1)}, bf16[128,2560]{1,0:T(8,128)(2,1)}, bf16[1,8,16,2560]{3,2,1,0:T(8,128)(2,1)}) conditional(s32[]{:T(128)} %clamp.3, (s32[20]{0:T(128)}, bf16[128,2560]{1,0:T(8,128)(2,1)}, bf16[128,2560]{1,0:T(8,128)(2,1)}, bf16[128,2560]{1,0:T(8,128)(2,1)}, ...), branch_computations={%region_1.0_spmd, %region_2.0_spmd, %region_3.0_spmd, %region_4.0_... | conditional | flops 1992294400 | bytes 78155880 | solution.py:503
  6.5 0.0 copy-start.21
  6.5 0.0 copy-start.29
  6.5 2.5 %branch_3_fun.9 = (s32[20]{0:T(128)S(1)}, bf16[2,16,2560]{2,1,0:T(8,128)(2,1)S(1)}, bf16[2,16,2560]{2,1,0:T(8,128)(2,1)S(1)}, bf16[10,2,128,128]{3,2,1,0:T(8,128)(2,1)S(1)}) custom-call(s32[20]{0:T(128)} %get-tuple-element.163.reach, bf16[128,2560]{1,0:T(8,128)(2,1)} %get-tuple-element.164.k, bf16[128,2560]{1,0:T(8,128)(2,1)} %get-tuple-element.165.v), custom_call_target="tpu_custom_call" | custom-call | bytes 2293920 | tf_op jit(solution)/shard_map/cond/branch_3_fun/pallas_call | solution.py:415
  9.1 0.0 copy-start.45
  9.1 2.6 %collective-permute-start.36 = (bf16[2,16,2560]{2,1,0:T(8,128)(2,1)S(1)}, bf16[2,16,2560]{2,1,0:T(8,128)(2,1)S(1)}, u32[]{:S(2)}, u32[]{:S(2)}) collective-permute-start(bf16[2,16,2560]{2,1,0:T(8,128)(2,1)S(1)} %get-tuple-element.169), channel_id=1, source_target_pairs={{0,1},{2,3},{4,5},{6,7},{8,9},{10,11},{12,13},{14,15},{1,0},{3,2},... | collective-permute-start | bytes 491528 | tf_op jit(solution)/shard_map/cond/branch_3_fun/ppermute | solution.py:32
  11.7 5.1 %collective-permute-start.37 = (bf16[2,16,2560]{2,1,0:T(8,128)(2,1)S(1)}, bf16[2,16,2560]{2,1,0:T(8,128)(2,1)S(1)}, u32[]{:S(2)}, u32[]{:S(2)}) collective-permute-start(bf16[2,16,2560]{2,1,0:T(8,128)(2,1)S(1)} %get-tuple-element.170), channel_id=1, source_target_pairs={{1,2},{3,4},{5,6},{7,8},{9,10},{11,12},{13,14},{2,1},{4,3},{6,5},{... | collective-permute-start | bytes 491528 | tf_op jit(solution)/shard_map/cond/branch_3_fun/ppermute | solution.py:32
  16.8 3.2 %collective-permute-start.40 = (bf16[10,2,128,128]{3,2,1,0:T(8,128)(2,1)S(1)}, bf16[10,2,128,128]{3,2,1,0:T(8,128)(2,1)S(1)}, u32[]{:S(2)}, u32[]{:S(2)}) collective-permute-start(bf16[10,2,128,128]{3,2,1,0:T(8,128)(2,1)S(1)} %get-tuple-element.168.own), channel_id=1, source_target_pairs={{0,16},{16,32},{32,48},{48,64},{64,80},{80,96},{96,112},{112,128},... | collective-permute-start | bytes 1966088 | tf_op jit(solution)/shard_map/cond/branch_3_fun/ppermute | solution.py:26
  20.0 4.2 %collective-permute-start.41 = (bf16[10,2,128,128]{3,2,1,0:T(8,128)(2,1)S(1)}, bf16[10,2,128,128]{3,2,1,0:T(8,128)(2,1)S(1)}, u32[]{:S(2)}, u32[]{:S(2)}) collective-permute-start(bf16[10,2,128,128]{3,2,1,0:T(8,128)(2,1)S(1)} %get-tuple-element.168.own), channel_id=1, source_target_pairs={{16,0},{32,16},{48,32},{64,48},{80,64},{96,80},{112,96},{128,112},... | collective-permute-start | bytes 1966088 | tf_op jit(solution)/shard_map/cond/branch_3_fun/ppermute | solution.py:26
  24.2 0.0 collective-permute-done.36.near
  24.2 0.0 collective-permute-done.37.far
  24.2 0.6 branch_3_fun.10.rims.own_r
  24.9 0.0 copy-done.21
  24.9 0.0 copy-done.29
  24.9 0.7 branch_3_fun.11.own_q
  25.6 1.9 %collective-permute-start.38 = (bf16[10,2,128,128]{3,2,1,0:T(8,128)(2,1)S(1)}, bf16[10,2,128,128]{3,2,1,0:T(8,128)(2,1)}, u32[]{:S(2)}, u32[]{:S(2)}) collective-permute-start(bf16[10,2,128,128]{3,2,1,0:T(8,128)(2,1)S(1)} %branch_3_fun.11.own_q), channel_id=1, source_target_pairs={{0,16},{16,32},{32,48},{48,64},{64,80},{80,96},{96,112},{112,128},... | collective-permute-start | bytes 1966088 | tf_op jit(solution)/shard_map/cond/branch_3_fun/ppermute | solution.py:26
  27.6 5.5 %collective-permute-start.39 = (bf16[10,2,128,128]{3,2,1,0:T(8,128)(2,1)S(1)}, bf16[10,2,128,128]{3,2,1,0:T(8,128)(2,1)}, u32[]{:S(2)}, u32[]{:S(2)}) collective-permute-start(bf16[10,2,128,128]{3,2,1,0:T(8,128)(2,1)S(1)} %branch_3_fun.11.own_q), channel_id=1, source_target_pairs={{16,0},{32,16},{48,32},{64,48},{80,64},{96,80},{112,96},{128,112},... | collective-permute-start | bytes 1966088 | tf_op jit(solution)/shard_map/cond/branch_3_fun/ppermute | solution.py:26
  33.0 1.9 %collective-permute-start.42 = (bf16[10,2,2,16,128]{4,3,2,1,0:T(8,128)(2,1)S(1)}, bf16[10,2,2,16,128]{4,3,2,1,0:T(8,128)(2,1)S(1)}, u32[]{:S(2)}, u32[]{:S(2)}) collective-permute-start(bf16[10,2,2,16,128]{4,3,2,1,0:T(8,128)(2,1)S(1)} %branch_3_fun.10.rims.own_r), channel_id=1, source_target_pairs={{0,16},{16,32},{32,48},{48,64},{64,80},{80,96},{96,112},{112,128},... | collective-permute-start | bytes 491528 | tf_op jit(solution)/shard_map/cond/branch_3_fun/ppermute | solution.py:26
  35.0 17.1 %collective-permute-done.42.prev_r = bf16[10,2,2,16,128]{4,3,2,1,0:T(8,128)(2,1)S(1)} collective-permute-done((bf16[10,2,2,16,128]{4,3,2,1,0:T(8,128)(2,1)S(1)}, bf16[10,2,2,16,128]{4,3,2,1,0:T(8,128)(2,1)S(1)}, u32[]{:S(2)}, u32[]{:S(2)}) %collective-permute-start.42) | collective-permute-done | bytes 163872 | tf_op jit(solution)/shard_map/cond/branch_3_fun/ppermute | solution.py:26
  52.1 3.2 %collective-permute-start.43 = (bf16[10,2,2,16,128]{4,3,2,1,0:T(8,128)(2,1)S(1)}, bf16[10,2,2,16,128]{4,3,2,1,0:T(8,128)(2,1)S(1)}, u32[]{:S(2)}, u32[]{:S(2)}) collective-permute-start(bf16[10,2,2,16,128]{4,3,2,1,0:T(8,128)(2,1)S(1)} %branch_3_fun.10.rims.own_r), channel_id=1, source_target_pairs={{16,0},{32,16},{48,32},{64,48},{80,64},{96,80},{112,96},{128,112},... | collective-permute-start | bytes 491528 | tf_op jit(solution)/shard_map/cond/branch_3_fun/ppermute | solution.py:26
  55.3 0.0 copy-done.45
  55.3 0.1 copy.12.offs
  55.4 0.0 copy-start.37
  55.4 5.4 %branch_3_fun.14 = (bf16[10,3,128,128]{3,2,1,0:T(8,128)(2,1)S(1)}, bf16[10,2,2,16,128]{4,3,2,1,0:T(8,128)(2,1)S(1)}) custom-call(s32[20]{0:T(128)S(1)} %get-tuple-element.166.order, s32[32,2]{1,0:T(8,128)S(1)} %copy.12.offs, bf16[128,2560]{1,0:T(8,128)(2,1)} %get-tuple-element.171.q, bf16[128,2560]{1,0:T(8,128)(2,1)} %get-tuple-element.172.g, ...), custom_call_target="tpu_custom_call" | custom-call | flops 262144000 | bytes 4096336 | tf_op jit(solution)/shard_map/cond/branch_3_fun/pallas_call | solution.py:415
  60.8 0.0 collective-permute-done.43.next_r
  60.8 0.0 collective-permute-done.40.prev
  60.8 0.0 collective-permute-done.41.following
  60.9 0.0 copy-done.37
  60.9 3.0 %branch_3_fun.12 = (f32[5,8,128]{2,1,0:T(8,128)S(1)}, f32[10,3,80,128]{3,2,1,0:T(8,128)S(1)}, f32[10,3,80,128]{3,2,1,0:T(8,128)S(1)}) custom-call(s32[20]{0:T(128)S(1)} %get-tuple-element.166.order, s32[20]{0:T(128)S(1)} %copy-done.37, s32[32,2]{1,0:T(8,128)S(1)} %copy.12.offs, bf16[10,2,128,128]{3,2,1,0:T(8,128)(2,1)S(1)} %branch_3_fun.11.own_q, ...), custom_call_target="tpu_custom_call" | custom-call | flops 314572800 | bytes 5591456 | tf_op jit(solution)/shard_map/cond/branch_3_fun/pallas_call | solution.py:415
  63.9 2.0 %collective-permute-start.44 = (f32[5,8,128]{2,1,0:T(8,128)S(1)}, f32[5,8,128]{2,1,0:T(8,128)S(1)}, u32[]{:S(2)}, u32[]{:S(2)}) collective-permute-start(f32[5,8,128]{2,1,0:T(8,128)S(1)} %get-tuple-element.173.stats), channel_id=1, source_target_pairs={{0,16},{16,32},{32,48},{48,64},{64,80},{80,96},{96,112},{112,128},... | collective-permute-start | bytes 61448 | tf_op jit(solution)/shard_map/cond/branch_3_fun/ppermute | solution.py:26
  65.9 5.4 %collective-permute-start.45 = (f32[5,8,128]{2,1,0:T(8,128)S(1)}, f32[5,8,128]{2,1,0:T(8,128)S(1)}, u32[]{:S(2)}, u32[]{:S(2)}) collective-permute-start(f32[5,8,128]{2,1,0:T(8,128)S(1)} %get-tuple-element.173.stats), channel_id=1, source_target_pairs={{16,0},{32,16},{48,32},{64,48},{80,64},{96,80},{112,96},{128,112},... | collective-permute-start | bytes 61448 | tf_op jit(solution)/shard_map/cond/branch_3_fun/ppermute | solution.py:26
  71.3 2.6 %branch_3_fun.13 = (f32[10,2,160,128]{3,2,1,0:T(8,128)S(1)}, bf16[10,128,128]{2,1,0:T(8,128)(2,1)S(1)}) custom-call(s32[20]{0:T(128)S(1)} %get-tuple-element.166.order, s32[20]{0:T(128)S(1)} %copy-done.37, s32[32,2]{1,0:T(8,128)S(1)} %copy.12.offs, bf16[10,2,128,128]{3,2,1,0:T(8,128)(2,1)S(1)} %branch_3_fun.11.own_q, ...), custom_call_target="tpu_custom_call" | custom-call | flops 262144000 | bytes 7557536 | tf_op jit(solution)/shard_map/cond/branch_3_fun/pallas_call | solution.py:415
  73.9 0.0 collective-permute-done.44.st_prev
  73.9 0.0 collective-permute-done.45.st_next
  74.0 0.0 collective-permute-done.38.q_prev
  74.0 0.0 collective-permute-done.39.q_next
  74.0 5.8 %branch_3_fun.15 = (bf16[10,2,128,128]{3,2,1,0:T(8,128)(2,1)S(1)}, bf16[2,16,2560]{2,1,0:T(8,128)(2,1)S(1)}, bf16[2,16,2560]{2,1,0:T(8,128)(2,1)S(1)}) custom-call(s32[20]{0:T(128)S(1)} %get-tuple-element.166.order, s32[20]{0:T(128)S(1)} %copy-done.37, s32[32,2]{1,0:T(8,128)S(1)} %copy.12.offs, bf16[10,2,128,128]{3,2,1,0:T(8,128)(2,1)S(1)} %get-tuple-element.168.own, ...), custom_call_target="tpu_custom_call" | custom-call | flops 419430400 | bytes 4956576 | tf_op jit(solution)/shard_map/cond/branch_3_fun/pallas_call | solution.py:415
  79.8 6.0 %collective-permute-start.46 = (bf16[2,16,2560]{2,1,0:T(8,128)(2,1)S(1)}, bf16[2,16,2560]{2,1,0:T(8,128)(2,1)S(1)}, u32[]{:S(2)}, u32[]{:S(2)}) collective-permute-start(bf16[2,16,2560]{2,1,0:T(8,128)(2,1)S(1)} %get-tuple-element.178), channel_id=1, source_target_pairs={{0,1},{1,2},{2,3},{3,4},{4,5},{5,6},{6,7},{7,8},{8,9},{9,10},{10,1... | collective-permute-start | bytes 491528 | tf_op jit(solution)/shard_map/cond/branch_3_fun/ppermute | solution.py:26
  85.8 1.9 %collective-permute-start.47 = (bf16[2,16,2560]{2,1,0:T(8,128)(2,1)S(1)}, bf16[2,16,2560]{2,1,0:T(8,128)(2,1)S(1)}, u32[]{:S(2)}, u32[]{:S(2)}) collective-permute-start(bf16[2,16,2560]{2,1,0:T(8,128)(2,1)S(1)} %get-tuple-element.179), channel_id=1, source_target_pairs={{1,0},{2,1},{3,2},{4,3},{5,4},{6,5},{7,6},{8,7},{9,8},{10,9},{11,1... | collective-permute-start | bytes 491528 | tf_op jit(solution)/shard_map/cond/branch_3_fun/ppermute | solution.py:26
  87.8 1.6 %branch_3_fun.17 = bf16[128,2560]{1,0:T(8,128)(2,1)} custom-call(s32[20]{0:T(128)S(1)} %get-tuple-element.166.order, bf16[10,128,128]{2,1,0:T(8,128)(2,1)S(1)} %get-tuple-element.184.refs_0_, bf16[10,3,128,128]{3,2,1,0:T(8,128)(2,1)S(1)} %get-tuple-element.181.refs_1_), custom_call_target="tpu_custom_call" | custom-call | bytes 1966160 | tf_op jit(solution)/shard_map/cond/branch_3_fun/pallas_call | solution.py:415
  89.3 0.0 collective-permute-done.46.below
  89.3 4.3 %collective-permute-done.47.above = bf16[2,16,2560]{2,1,0:T(8,128)(2,1)S(1)} collective-permute-done((bf16[2,16,2560]{2,1,0:T(8,128)(2,1)S(1)}, bf16[2,16,2560]{2,1,0:T(8,128)(2,1)S(1)}, u32[]{:S(2)}, u32[]{:S(2)}) %collective-permute-start.47) | collective-permute-done | bytes 163872 | tf_op jit(solution)/shard_map/cond/branch_3_fun/ppermute | solution.py:26
  93.7 1.9 %branch_3_fun.16 = (bf16[128,2560]{1,0:T(8,128)(2,1)}, bf16[128,2560]{1,0:T(8,128)(2,1)}) custom-call(s32[20]{0:T(128)S(1)} %get-tuple-element.166.order, bf16[2,16,2560]{2,1,0:T(8,128)(2,1)S(1)} %collective-permute-done.46.below, bf16[2,16,2560]{2,1,0:T(8,128)(2,1)S(1)} %collective-permute-done.47.above, ...), custom_call_target="tpu_custom_call" | custom-call | bytes 3276880 | tf_op jit(solution)/shard_map/cond/branch_3_fun/pallas_call | solution.py:415
Async XLA Ops:
  6.5 18.4 %copy-start.21 = (bf16[128,2560]{1,0:T(8,128)(2,1)S(1)}, bf16[128,2560]{1,0:T(8,128)(2,1)}, u32[]{:S(2)}) copy-start(bf16[128,2560]{1,0:T(8,128)(2,1)} %get-tuple-element.171.q) | copy-start | bytes 1966084 | tf_op jit(solution)/shard_map/cond
  6.5 18.4 %copy-start.29 = (bf16[128,2560]{1,0:T(8,128)(2,1)S(1)}, bf16[128,2560]{1,0:T(8,128)(2,1)}, u32[]{:S(2)}) copy-start(bf16[128,2560]{1,0:T(8,128)(2,1)} %get-tuple-element.172.g) | copy-start | bytes 1966084 | tf_op jit(solution)/shard_map/cond
  9.1 46.3 %copy-start.45 = (s32[32,2]{0,1:T(2,128)S(1)}, s32[32,2]{0,1:T(2,128)}, u32[]{:S(2)}) copy-start(s32[32,2]{0,1:T(2,128)} %get-tuple-element.303) | copy-start | bytes 772 | tf_op jit(solution)/shard_map/cond
  9.1 15.1 %collective-permute-start.36 = (bf16[2,16,2560]{2,1,0:T(8,128)(2,1)S(1)}, bf16[2,16,2560]{2,1,0:T(8,128)(2,1)S(1)}, u32[]{:S(2)}, u32[]{:S(2)}) collective-permute-start(bf16[2,16,2560]{2,1,0:T(8,128)(2,1)S(1)} %get-tuple-element.169), channel_id=1, source_target_pairs={{0,1},{2,3},{4,5},{6,7},{8,9},{10,11},{12,13},{14,15},{1,0},{3,2},... | collective-permute-start | bytes 491528 | tf_op jit(solution)/shard_map/cond/branch_3_fun/ppermute | solution.py:32
  11.7 12.5 %collective-permute-start.37 = (bf16[2,16,2560]{2,1,0:T(8,128)(2,1)S(1)}, bf16[2,16,2560]{2,1,0:T(8,128)(2,1)S(1)}, u32[]{:S(2)}, u32[]{:S(2)}) collective-permute-start(bf16[2,16,2560]{2,1,0:T(8,128)(2,1)S(1)} %get-tuple-element.170), channel_id=1, source_target_pairs={{1,2},{3,4},{5,6},{7,8},{9,10},{11,12},{13,14},{2,1},{4,3},{6,5},{... | collective-permute-start | bytes 491528 | tf_op jit(solution)/shard_map/cond/branch_3_fun/ppermute | solution.py:32
  16.8 44.1 %collective-permute-start.40 = (bf16[10,2,128,128]{3,2,1,0:T(8,128)(2,1)S(1)}, bf16[10,2,128,128]{3,2,1,0:T(8,128)(2,1)S(1)}, u32[]{:S(2)}, u32[]{:S(2)}) collective-permute-start(bf16[10,2,128,128]{3,2,1,0:T(8,128)(2,1)S(1)} %get-tuple-element.168.own), channel_id=1, source_target_pairs={{0,16},{16,32},{32,48},{48,64},{64,80},{80,96},{96,112},{112,128},... | collective-permute-start | bytes 1966088 | tf_op jit(solution)/shard_map/cond/branch_3_fun/ppermute | solution.py:26
  20.0 40.9 %collective-permute-start.41 = (bf16[10,2,128,128]{3,2,1,0:T(8,128)(2,1)S(1)}, bf16[10,2,128,128]{3,2,1,0:T(8,128)(2,1)S(1)}, u32[]{:S(2)}, u32[]{:S(2)}) collective-permute-start(bf16[10,2,128,128]{3,2,1,0:T(8,128)(2,1)S(1)} %get-tuple-element.168.own), channel_id=1, source_target_pairs={{16,0},{32,16},{48,32},{64,48},{80,64},{96,80},{112,96},{128,112},... | collective-permute-start | bytes 1966088 | tf_op jit(solution)/shard_map/cond/branch_3_fun/ppermute | solution.py:26
  25.6 48.3 %collective-permute-start.38 = (bf16[10,2,128,128]{3,2,1,0:T(8,128)(2,1)S(1)}, bf16[10,2,128,128]{3,2,1,0:T(8,128)(2,1)}, u32[]{:S(2)}, u32[]{:S(2)}) collective-permute-start(bf16[10,2,128,128]{3,2,1,0:T(8,128)(2,1)S(1)} %branch_3_fun.11.own_q), channel_id=1, source_target_pairs={{0,16},{16,32},{32,48},{48,64},{64,80},{80,96},{96,112},{112,128},... | collective-permute-start | bytes 1966088 | tf_op jit(solution)/shard_map/cond/branch_3_fun/ppermute | solution.py:26
  27.6 46.4 %collective-permute-start.39 = (bf16[10,2,128,128]{3,2,1,0:T(8,128)(2,1)S(1)}, bf16[10,2,128,128]{3,2,1,0:T(8,128)(2,1)}, u32[]{:S(2)}, u32[]{:S(2)}) collective-permute-start(bf16[10,2,128,128]{3,2,1,0:T(8,128)(2,1)S(1)} %branch_3_fun.11.own_q), channel_id=1, source_target_pairs={{16,0},{32,16},{48,32},{64,48},{80,64},{96,80},{112,96},{128,112},... | collective-permute-start | bytes 1966088 | tf_op jit(solution)/shard_map/cond/branch_3_fun/ppermute | solution.py:26
  33.0 19.0 %collective-permute-start.42 = (bf16[10,2,2,16,128]{4,3,2,1,0:T(8,128)(2,1)S(1)}, bf16[10,2,2,16,128]{4,3,2,1,0:T(8,128)(2,1)S(1)}, u32[]{:S(2)}, u32[]{:S(2)}) collective-permute-start(bf16[10,2,2,16,128]{4,3,2,1,0:T(8,128)(2,1)S(1)} %branch_3_fun.10.rims.own_r), channel_id=1, source_target_pairs={{0,16},{16,32},{32,48},{48,64},{64,80},{80,96},{96,112},{112,128},... | collective-permute-start | bytes 491528 | tf_op jit(solution)/shard_map/cond/branch_3_fun/ppermute | solution.py:26
  52.1 8.7 %collective-permute-start.43 = (bf16[10,2,2,16,128]{4,3,2,1,0:T(8,128)(2,1)S(1)}, bf16[10,2,2,16,128]{4,3,2,1,0:T(8,128)(2,1)S(1)}, u32[]{:S(2)}, u32[]{:S(2)}) collective-permute-start(bf16[10,2,2,16,128]{4,3,2,1,0:T(8,128)(2,1)S(1)} %branch_3_fun.10.rims.own_r), channel_id=1, source_target_pairs={{16,0},{32,16},{48,32},{64,48},{80,64},{96,80},{112,96},{128,112},... | collective-permute-start | bytes 491528 | tf_op jit(solution)/shard_map/cond/branch_3_fun/ppermute | solution.py:26
  55.4 5.4 %copy-start.37 = (s32[20]{0:T(128)S(1)}, s32[20]{0:T(128)}, u32[]{:S(2)}) copy-start(s32[20]{0:T(128)} %get-tuple-element.163.reach) | copy-start | bytes 244 | tf_op jit(solution)/shard_map/cond
  63.9 10.0 %collective-permute-start.44 = (f32[5,8,128]{2,1,0:T(8,128)S(1)}, f32[5,8,128]{2,1,0:T(8,128)S(1)}, u32[]{:S(2)}, u32[]{:S(2)}) collective-permute-start(f32[5,8,128]{2,1,0:T(8,128)S(1)} %get-tuple-element.173.stats), channel_id=1, source_target_pairs={{0,16},{16,32},{32,48},{48,64},{64,80},{80,96},{96,112},{112,128},... | collective-permute-start | bytes 61448 | tf_op jit(solution)/shard_map/cond/branch_3_fun/ppermute | solution.py:26
  65.9 8.0 %collective-permute-start.45 = (f32[5,8,128]{2,1,0:T(8,128)S(1)}, f32[5,8,128]{2,1,0:T(8,128)S(1)}, u32[]{:S(2)}, u32[]{:S(2)}) collective-permute-start(f32[5,8,128]{2,1,0:T(8,128)S(1)} %get-tuple-element.173.stats), channel_id=1, source_target_pairs={{16,0},{32,16},{48,32},{64,48},{80,64},{96,80},{112,96},{128,112},... | collective-permute-start | bytes 61448 | tf_op jit(solution)/shard_map/cond/branch_3_fun/ppermute | solution.py:26
  79.8 9.5 %collective-permute-start.46 = (bf16[2,16,2560]{2,1,0:T(8,128)(2,1)S(1)}, bf16[2,16,2560]{2,1,0:T(8,128)(2,1)S(1)}, u32[]{:S(2)}, u32[]{:S(2)}) collective-permute-start(bf16[2,16,2560]{2,1,0:T(8,128)(2,1)S(1)} %get-tuple-element.178), channel_id=1, source_target_pairs={{0,1},{1,2},{2,3},{3,4},{4,5},{5,6},{6,7},{7,8},{8,9},{9,10},{10,1... | collective-permute-start | bytes 491528 | tf_op jit(solution)/shard_map/cond/branch_3_fun/ppermute | solution.py:26
  85.8 7.8 %collective-permute-start.47 = (bf16[2,16,2560]{2,1,0:T(8,128)(2,1)S(1)}, bf16[2,16,2560]{2,1,0:T(8,128)(2,1)S(1)}, u32[]{:S(2)}, u32[]{:S(2)}) collective-permute-start(bf16[2,16,2560]{2,1,0:T(8,128)(2,1)S(1)} %get-tuple-element.179), channel_id=1, source_target_pairs={{1,0},{2,1},{3,2},{4,3},{5,4},{6,5},{7,6},{8,7},{9,8},{10,9},{11,1... | collective-permute-start | bytes 491528 | tf_op jit(solution)/shard_map/cond/branch_3_fun/ppermute | solution.py:26
